TPU v7x, 256 devices: a whole 4x4x8 slice. The times are simulated.
256 devices in a mesh: snap: 4 (over x), dom: 64 (over y, z, core).
Axes of the slice: x: 4, y: 4, z: 8, core: 2. Of those that a mesh axis runs over, the one named last changes fastest.
Arguments:
- readings: bfloat16 [4, 2, 32768], P('snap', None, 'dom'), may hold values from -6 to 6
- previous: bfloat16 [4, 64, 32768], P('snap', None, 'dom'), may hold values from -3 to 3
- upstream: bfloat16 [4, 64, 32768], P('snap', None, 'dom'), may hold values from -6 to 6
- gate_weight: bfloat16 [128, 330], replicated, may hold values from -0.3125 to 0.3125
- gate_bias: float32 [128], replicated, may hold values from -4 to 4
- cand_weight: bfloat16 [64, 330], replicated, may hold values from -0.3125 to 0.3125
- cand_bias: float32 [64], replicated, may hold values from -3 to 3
- neighbours: int32 [4, 32768], P(None, 'dom'), may hold values from 0 to 767, as said below
- edge_weight: float32 [4, 32768], P(None, 'dom'), may hold values from 0.1 to 1
- send_rows: int32 [64, 256], P('dom'), may hold values from 0 to 511, as said below
Outputs:
- state_grad: bfloat16 [4, 64, 32768], P('snap', None, 'dom')
- gate_weight_grad: float32 [128, 330], replicated
- gate_bias_grad: float32 [128], replicated
- cand_weight_grad: float32 [64, 330], replicated
- cand_bias_grad: float32 [64], replicated
Inputs may be any that keep to these rules, and one draw needn't show every extreme that they name: Value v of neighbours[d, i] below 512 is a row of segment i's own partition; v = 512 + q * 4 + s names slot s of what partition q sends to segment i's partition. Row d = 0 names each row of a partition exactly once, and in every partition every value from 512 to 767 appears. `send_rows`: row q holds rows of partition q; slots p * 4 to p * 4 + 3 are those sent to partition p; rows may repeat.
All inputs are finite; a program needn't handle non-finite values.
Results may differ from a plain program's by a relative error of at most 0.006.
Values may be sent and summed in bfloat16 or wider, within the bound.
A program may use at most 64 MiB of HBM per device.

v0:
```python
import math

import jax
import jax.numpy as jnp
from jax import lax
from jax.sharding import PartitionSpec as P


def collect(extended, weights, index):
    total = jnp.zeros(extended.shape[:2] + (index.shape[1],), jnp.float32)
    for slot in range(index.shape[0]):
        total = total + jnp.take(extended, index[slot], axis=2).astype(jnp.float32) * weights[slot]
    return total


def spread(values, weights, index, width):
    total = jnp.zeros(values.shape[:2] + (width,), jnp.float32)
    for slot in range(index.shape[0]):
        total = total.at[:, :, index[slot]].add(values.astype(jnp.float32) * weights[slot])
    return total


def pull(values, weights, index, sender, move):
    arrived = move(jnp.take(values, sender, axis=2))
    return collect(jnp.concatenate([values, arrived], axis=2), weights, index)


def push(values, weights, index, sender, move):
    width = values.shape[2]
    total = spread(values, weights, index, width + sender.shape[0])
    returned = move(total[:, :, width:])
    return total[:, :, :width].at[:, :, sender].add(returned)


def diffuse(base, walk_out, walk_in, index, sender, moves):
    lower = base.astype(jnp.float32)
    first_out = push(base, walk_out, index, sender, moves[1]).astype(jnp.bfloat16)
    second_out = push(first_out, walk_out, index, sender, moves[1])
    first_in = pull(base, walk_in, index, sender, moves[0]).astype(jnp.bfloat16)
    second_in = pull(first_in, walk_in, index, sender, moves[0])
    second_out = (2.0 * second_out - lower).astype(jnp.bfloat16)
    second_in = (2.0 * second_in - lower).astype(jnp.bfloat16)
    return jnp.concatenate([base, first_out, second_out, first_in, second_in], axis=1)


def adjoint(grads, walk_out, walk_in, index, sender, moves):
    pulled = pull(grads[:, 2], walk_out, index, sender, moves[0])
    pushed = push(grads[:, 4], walk_in, index, sender, moves[1])
    turned_out = (grads[:, 1].astype(jnp.float32) + 2.0 * pulled).astype(jnp.bfloat16)
    turned_in = (grads[:, 3].astype(jnp.float32) + 2.0 * pushed).astype(jnp.bfloat16)
    pulled_last = pull(turned_out, walk_out, index, sender, moves[0])
    pushed_last = push(turned_in, walk_in, index, sender, moves[1])
    direct = (
        grads[:, 0].astype(jnp.float32)
        - grads[:, 2].astype(jnp.float32)
        - grads[:, 4].astype(jnp.float32)
    )
    return direct + pulled_last + pushed_last


def body(
    readings,
    previous,
    upstream,
    gate_weight,
    gate_bias,
    cand_weight,
    cand_bias,
    neighbours,
    edge_weight,
    send_rows,
):
    inputs = readings.shape[1]
    hidden = previous.shape[1]
    chans = inputs + hidden
    orders = gate_weight.shape[1] // chans
    snaps = readings.shape[0]
    width = readings.shape[2]
    sender = send_rows[0]
    state_moves = (
        lambda buffer: lax.all_to_all(buffer, "dom", split_axis=2, concat_axis=2, tiled=True),
        lambda buffer: lax.all_to_all(buffer, "dom", split_axis=2, concat_axis=2, tiled=True),
    )
    reset_moves = (
        lambda buffer: lax.all_to_all(buffer, "dom", split_axis=2, concat_axis=2, tiled=True),
        lambda buffer: lax.all_to_all(
            buffer.astype(jnp.bfloat16), "dom", split_axis=2, concat_axis=2, tiled=True
        ).astype(buffer.dtype),
    )
    adjoint_moves = (
        lambda buffer: lax.all_to_all(buffer, "dom", split_axis=2, concat_axis=2, tiled=True),
        lambda buffer: lax.all_to_all(
            buffer.astype(jnp.bfloat16), "dom", split_axis=2, concat_axis=2, tiled=True
        ).astype(buffer.dtype),
    )
    unity = jnp.ones((1, 1, width), jnp.float32)
    out_degree = push(
        unity,
        edge_weight,
        neighbours,
        sender,
        lambda buffer: lax.all_to_all(buffer, "dom", split_axis=2, concat_axis=2, tiled=True),
    )
    source_degree = lax.all_to_all(
        jnp.take(out_degree, sender, axis=2), "dom", split_axis=2, concat_axis=2, tiled=True
    )
    degree_table = jnp.concatenate([out_degree, source_degree], axis=2)[0, 0]
    walk_out = edge_weight / jnp.take(degree_table, neighbours)
    walk_in = edge_weight / jnp.sum(edge_weight, axis=0)[None, :]
    base = jnp.concatenate([readings, previous], axis=1)
    states = diffuse(base, walk_out, walk_in, neighbours, sender, state_moves)
    gates = (
        jnp.einsum("ok,skn->son", gate_weight, states, preferred_element_type=jnp.float32)
        + gate_bias[None, :, None]
    )
    reset = jax.nn.sigmoid(gates[:, :hidden])
    update = jax.nn.sigmoid(gates[:, hidden:])
    held = previous.astype(jnp.float32)
    scaled = (reset * held).astype(jnp.bfloat16)
    scaled_hops = diffuse(scaled, walk_out, walk_in, neighbours, sender, reset_moves)
    input_hops = states.reshape(snaps, orders, chans, width)[:, :, :inputs]
    mixed = jnp.concatenate(
        [input_hops, scaled_hops.reshape(snaps, orders, hidden, width)], axis=2
    ).reshape(snaps, orders * chans, width)
    cand = jnp.tanh(
        jnp.einsum("ok,skn->son", cand_weight, mixed, preferred_element_type=jnp.float32)
        + cand_bias[None, :, None]
    )
    upward = upstream.astype(jnp.float32)
    cand_grad = (upward * (1.0 - update) * (1.0 - cand * cand)).astype(jnp.bfloat16)
    part_wc = jnp.einsum("son,skn->ok", cand_grad, mixed, preferred_element_type=jnp.float32)
    part_bc = jnp.sum(cand_grad.astype(jnp.float32), axis=(0, 2))
    cand_sums = (part_wc, part_bc)
    cand_rows = cand_weight.reshape(hidden, orders, chans)[:, :, inputs:].reshape(
        hidden, orders * hidden
    )
    back_c = jnp.einsum("ok,son->skn", cand_rows, cand_grad, preferred_element_type=jnp.float32)
    back_c = back_c.astype(jnp.bfloat16).reshape(snaps, orders, hidden, width)
    scaled_grad = adjoint(back_c, walk_out, walk_in, neighbours, sender, adjoint_moves)
    reset_part = scaled_grad * held * reset * (1.0 - reset)
    update_part = upward * (held - cand) * update * (1.0 - update)
    gate_grad = jnp.concatenate([reset_part, update_part], axis=1).astype(jnp.bfloat16)
    part_wru = jnp.einsum("son,skn->ok", gate_grad, states, preferred_element_type=jnp.float32)
    part_bru = jnp.sum(gate_grad.astype(jnp.float32), axis=(0, 2))
    gate_rows = gate_weight.reshape(2 * hidden, orders, chans)[:, :, inputs:].reshape(
        2 * hidden, orders * hidden
    )
    back_g = jnp.einsum("ok,son->skn", gate_rows, gate_grad, preferred_element_type=jnp.float32)
    back_g = back_g.astype(jnp.bfloat16).reshape(snaps, orders, hidden, width)
    state_part = adjoint(back_g, walk_out, walk_in, neighbours, sender, adjoint_moves)
    state_grad = (upward * update + scaled_grad * reset + state_part).astype(jnp.bfloat16)
    grad_wru, grad_bru, grad_wc, grad_bc = lax.psum(
        (part_wru, part_bru, cand_sums[0], cand_sums[1]), ("snap", "dom")
    )
    factor = 1.0 / math.sqrt(snaps * lax.axis_size("snap") * width * lax.axis_size("dom"))
    return (state_grad, grad_wru * factor, grad_bru * factor, grad_wc * factor, grad_bc * factor)


def solution(mesh):
    in_specs = (
        P("snap", None, "dom"),
        P("snap", None, "dom"),
        P("snap", None, "dom"),
        P(),
        P(),
        P(),
        P(),
        P(None, "dom"),
        P(None, "dom"),
        P("dom", None),
    )
    out_specs = (P("snap", None, "dom"), P(), P(), P(), P())
    return jax.shard_map(body, mesh=mesh, in_specs=in_specs, out_specs=out_specs, check_vma=False)
```

profile of v0, /device:TPU:1, one launch (start us, length us, event | category | flops | bytes accessed | tf_op | source)
XLA Modules:
  0.0 777.2 jit_solution(16979545902675610887)
XLA Ops:
  12.2 4.1 scatter_fusion
  16.3 4.1 scatter_fusion.1
  25.3 13.3 %all-to-all-start = ((f32[1,1,256]{1,0,2:T(1,128)}), f32[1,1,256]{1,0,2:T(1,128)S(1)}, u32[]{:S(2)}, u32[]{:S(2)}) async-start(f32[1,1,256]{1,0,2:T(1,128)} %copy.339), calls=%async_computation | async-start | bytes 262144 | tf_op jit(solution)/shard_map/all_to_all | solution.py:102
  42.2 6.7 all-to-all-done
  55.0 4.9 all-to-all-start.1
  62.5 7.8 all-to-all-done.1
  70.3 4.9 all-to-all-start.4
  75.3 8.6 %gather_fusion.1 = f32[2048]{0:T(1024)S(1)} fusion(f32[768]{0:T(1024)S(1)} %maximum_reduce_fusion, s32[2048]{0:T(1024)S(1)} %broadcast_clamp_fusion), kind=kCustom, calls=%fused_computation.41 | custom fusion | bytes 24576 | tf_op jit(solution)/shard_map/jit(_take)/gather | solution.py:108
  94.3 9.3 %all-to-all-start.5 = ((bf16[64,2,132]{2,1,0:T(2,128)(2,1)}), bf16[64,2,132]{2,1,0:T(2,128)(2,1)S(1)}, u32[]{:S(2)}, u32[]{:S(2)}) async-start(bf16[64,2,132]{2,1,0:T(2,128)(2,1)} %reshape.2272), calls=%async_computation.5 | async-start | bytes 131072 | tf_op jit(solution)/shard_map/all_to_all | solution.py:81
  117.9 10.3 %all-to-all-start.2 = ((f32[1,66,256]{1,0,2:T(1,128)}), f32[1,66,256]{1,0,2:T(1,128)S(1)}, u32[]{:S(2)}, u32[]{:S(2)}) async-start(f32[1,66,256]{1,0,2:T(1,128)} %bitcast.32), calls=%async_computation.2 | async-start | bytes 262144 | tf_op jit(solution)/shard_map/all_to_all | solution.py:82
  133.8 4.7 all-to-all-done.2
  155.0 5.6 all-to-all-start.3
  160.6 10.3 %all-to-all-done.3 = f32[1,66,256]{1,0,2:T(1,128)S(1)} async-done(((f32[1,66,256]{1,0,2:T(1,128)}), f32[1,66,256]{1,0,2:T(1,128)S(1)}, u32[]{:S(2)}, u32[]{:S(2)}) %all-to-all-start.3) | async-done | bytes 67616 | tf_op jit(solution)/shard_map/all_to_all | solution.py:82
  190.5 4.9 all-to-all-start.6
  198.4 6.2 all-to-all-done.6
  204.6 4.7 all-to-all-start.8
  227.2 11.0 %all-to-all-start.7 = ((bf16[64,2,128]{2,1,0:T(2,128)(2,1)}), bf16[64,2,128]{2,1,0:T(2,128)(2,1)S(1)}, u32[]{:S(2)}, u32[]{:S(2)}) async-start(bf16[64,2,128]{2,1,0:T(2,128)(2,1)} %reshape.2276), calls=%async_computation.7 | async-start | bytes 65536 | tf_op jit(solution)/shard_map/all_to_all | solution.py:86
  252.9 7.3 all-to-all-start.9
  261.6 7.9 %all-to-all-done.9 = bf16[64,2,128]{2,1,0:T(2,128)(2,1)S(1)} async-done(((bf16[64,2,128]{2,1,0:T(2,128)(2,1)}), bf16[64,2,128]{2,1,0:T(2,128)(2,1)S(1)}, u32[]{:S(2)}, u32[]{:S(2)}) %all-to-all-start.9) | async-done | bytes 32800 | tf_op jit(solution)/shard_map/all_to_all | solution.py:85
  281.2 5.0 all-to-all-start.10
  286.3 9.2 %all-to-all-done.10 = bf16[64,2,128]{2,1,0:T(2,128)(2,1)S(1)} async-done(((bf16[64,2,128]{2,1,0:T(2,128)(2,1)}), bf16[64,2,128]{2,1,0:T(2,128)(2,1)S(1)}, u32[]{:S(2)}, u32[]{:S(2)}) %all-to-all-start.10) | async-done | bytes 32800 | tf_op jit(solution)/shard_map/all_to_all | solution.py:91
  307.5 4.7 all-to-all-start.11
  324.8 10.4 %all-to-all-start.12 = ((bf16[64,2,128]{2,1,0:T(2,128)(2,1)}), bf16[64,2,128]{2,1,0:T(2,128)(2,1)S(1)}, u32[]{:S(2)}, u32[]{:S(2)}) async-start(bf16[64,2,128]{2,1,0:T(2,128)(2,1)} %reshape.2282), calls=%async_computation.12 | async-start | bytes 65536 | tf_op jit(solution)/shard_map/all_to_all | solution.py:92
  363.1 6.9 all-to-all-start.13
  370.3 9.0 %all-to-all-done.13 = bf16[64,2,128]{2,1,0:T(2,128)(2,1)S(1)} async-done(((bf16[64,2,128]{2,1,0:T(2,128)(2,1)}), bf16[64,2,128]{2,1,0:T(2,128)(2,1)S(1)}, u32[]{:S(2)}, u32[]{:S(2)}) %all-to-all-start.13) | async-done | bytes 32800 | tf_op jit(solution)/shard_map/all_to_all | solution.py:92
  386.1 4.7 all-to-all-start.14
  390.8 77.8 %all-reduce = (f32[128]{0:T(128)S(1)}, f32[64]{0:T(128)S(1)}) all-reduce(f32[128]{0:T(128)S(1)} %convert_reduce_fusion, f32[64]{0:T(128)S(1)} %get-tuple-element.33), channel_id=1, replica_groups=mesh['snap'=4,'dom'=64] {'snap','dom'}, use_global_device_ids=true, to_apply=%region_48.53 | all-reduce | flops 192 | bytes 1536 | tf_op jit(solution)/shard_map/psum | solution.py:152
  494.4 7.7 all-to-all-start.15
  502.2 211.7 %all-reduce.4.cloned.1.call-done = (f32[128,330]{0,1:T(8,128)}, f32[64,330]{1,0:T(8,128)}) async-done(((f32[128,330]{0,1:T(8,128)}, f32[64,330]{1,0:T(8,128)}), (f32[128,330]{0,1:T(8,128)}, f32[64,330]{1,0:T(8,128)})) %all-reduce.4.cloned.1.call-update) | async-done | bytes 253456 | tf_op jit(solution)/shard_map/psum | solution.py:152
  716.1 6.8 all-to-all-start.16
  750.8 6.9 all-to-all-start.17
  757.9 8.9 %all-to-all-done.17 = bf16[64,2,128]{2,1,0:T(2,128)(2,1)S(1)} async-done(((bf16[64,2,128]{2,1,0:T(2,128)(2,1)}), bf16[64,2,128]{2,1,0:T(2,128)(2,1)S(1)}, u32[]{:S(2)}, u32[]{:S(2)}) %all-to-all-start.17) | async-done | bytes 32800 | tf_op jit(solution)/shard_map/all_to_all | solution.py:92
  (373 shorter events, 254.1 us)
Async XLA Ops:
  7.2 0.9 copy-start.5
  24.5 17.7 %copy-start = (f32[1,1,768]{2,1,0:T(1,128)}, f32[1,1,768]{2,1,0:T(1,128)S(1)}, u32[]{:S(2)}) copy-start(f32[1,1,768]{2,1,0:T(1,128)S(1)} %reshape.1574) | copy-start | bytes 9220
  25.3 13.3 %copy-start.3 = (s32[4,512]{1,0:T(4,128)S(1)}, s32[4,512]{1,0:T(4,128)}, u32[]{:S(2)}) copy-start(s32[4,512]{1,0:T(4,128)} %param.25) | copy-start | bytes 24580
  25.3 23.6 %all-to-all-start = ((f32[1,1,256]{1,0,2:T(1,128)}), f32[1,1,256]{1,0,2:T(1,128)S(1)}, u32[]{:S(2)}, u32[]{:S(2)}) async-start(f32[1,1,256]{1,0,2:T(1,128)} %copy.339), calls=%async_computation | async-start | bytes 262144 | tf_op jit(solution)/shard_map/all_to_all | solution.py:102
  38.6 0.7 copy-start.8
  39.4 0.7 copy-start.9
  40.1 0.8 copy-start.1
  48.9 1.0 slice-start
  55.0 15.2 %all-to-all-start.1 = ((f32[1,1,256]{1,0,2:T(1,128)}), f32[1,1,256]{1,0,2:T(1,128)S(1)}, u32[]{:S(2)}, u32[]{:S(2)}) async-start(f32[1,1,256]{1,0,2:T(1,128)} %copy.340), calls=%async_computation.1 | async-start | bytes 262144 | tf_op jit(solution)/shard_map/all_to_all | solution.py:104
  70.3 14.7 %all-to-all-start.4 = ((bf16[64,2,132]{2,1,0:T(2,128)(2,1)}), bf16[64,2,132]{2,1,0:T(2,128)(2,1)S(1)}, u32[]{:S(2)}, u32[]{:S(2)}) async-start(bf16[64,2,132]{2,1,0:T(2,128)(2,1)} %reshape.2270), calls=%async_computation.4 | async-start | bytes 131072 | tf_op jit(solution)/shard_map/all_to_all | solution.py:81
  94.3 23.6 %all-to-all-start.5 = ((bf16[64,2,132]{2,1,0:T(2,128)(2,1)}), bf16[64,2,132]{2,1,0:T(2,128)(2,1)S(1)}, u32[]{:S(2)}, u32[]{:S(2)}) async-start(bf16[64,2,132]{2,1,0:T(2,128)(2,1)} %reshape.2272), calls=%async_computation.5 | async-start | bytes 131072 | tf_op jit(solution)/shard_map/all_to_all | solution.py:81
  117.9 20.7 %all-to-all-start.2 = ((f32[1,66,256]{1,0,2:T(1,128)}), f32[1,66,256]{1,0,2:T(1,128)S(1)}, u32[]{:S(2)}, u32[]{:S(2)}) async-start(f32[1,66,256]{1,0,2:T(1,128)} %bitcast.32), calls=%async_computation.2 | async-start | bytes 262144 | tf_op jit(solution)/shard_map/all_to_all | solution.py:82
  155.0 16.0 %all-to-all-start.3 = ((f32[1,66,256]{1,0,2:T(1,128)}), f32[1,66,256]{1,0,2:T(1,128)S(1)}, u32[]{:S(2)}, u32[]{:S(2)}) async-start(f32[1,66,256]{1,0,2:T(1,128)} %bitcast.46), calls=%async_computation.3 | async-start | bytes 262144 | tf_op jit(solution)/shard_map/all_to_all | solution.py:82
  173.8 0.9 copy-start.2
  173.8 0.9 copy-start.10
  190.5 14.1 %all-to-all-start.6 = ((bf16[64,2,128]{2,1,0:T(2,128)(2,1)}), bf16[64,2,128]{2,1,0:T(2,128)(2,1)S(1)}, u32[]{:S(2)}, u32[]{:S(2)}) async-start(bf16[64,2,128]{2,1,0:T(2,128)(2,1)} %reshape.2274), calls=%async_computation.6 | async-start | bytes 65536 | tf_op jit(solution)/shard_map/all_to_all | solution.py:86
  204.6 22.6 %all-to-all-start.8 = ((bf16[64,2,128]{2,1,0:T(2,128)(2,1)}), bf16[64,2,128]{2,1,0:T(2,128)(2,1)S(1)}, u32[]{:S(2)}, u32[]{:S(2)}) async-start(bf16[64,2,128]{2,1,0:T(2,128)(2,1)} %reshape.2278), calls=%async_computation.8 | async-start | bytes 65536 | tf_op jit(solution)/shard_map/all_to_all | solution.py:85
  227.2 20.2 %all-to-all-start.7 = ((bf16[64,2,128]{2,1,0:T(2,128)(2,1)}), bf16[64,2,128]{2,1,0:T(2,128)(2,1)S(1)}, u32[]{:S(2)}, u32[]{:S(2)}) async-start(bf16[64,2,128]{2,1,0:T(2,128)(2,1)} %reshape.2276), calls=%async_computation.7 | async-start | bytes 65536 | tf_op jit(solution)/shard_map/all_to_all | solution.py:86
  252.9 16.6 %all-to-all-start.9 = ((bf16[64,2,128]{2,1,0:T(2,128)(2,1)}), bf16[64,2,128]{2,1,0:T(2,128)(2,1)S(1)}, u32[]{:S(2)}, u32[]{:S(2)}) async-start(bf16[64,2,128]{2,1,0:T(2,128)(2,1)} %reshape.2280), calls=%async_computation.9 | async-start | bytes 65536 | tf_op jit(solution)/shard_map/all_to_all | solution.py:85
  260.3 0.8 copy-start.7
  275.9 0.8 copy-start.6
  275.9 0.8 copy-start.11
  281.2 14.3 %all-to-all-start.10 = ((bf16[64,2,128]{2,1,0:T(2,128)(2,1)}), bf16[64,2,128]{2,1,0:T(2,128)(2,1)S(1)}, u32[]{:S(2)}, u32[]{:S(2)}) async-start(bf16[64,2,128]{2,1,0:T(2,128)(2,1)} %reshape.2284), calls=%async_computation.10 | async-start | bytes 65536 | tf_op jit(solution)/shard_map/all_to_all | solution.py:91
  307.5 17.2 %all-to-all-start.11 = ((bf16[64,2,128]{2,1,0:T(2,128)(2,1)}), bf16[64,2,128]{2,1,0:T(2,128)(2,1)S(1)}, u32[]{:S(2)}, u32[]{:S(2)}) async-start(bf16[64,2,128]{2,1,0:T(2,128)(2,1)} %reshape.2286), calls=%async_computation.11 | async-start | bytes 65536 | tf_op jit(solution)/shard_map/all_to_all | solution.py:91
  324.8 19.7 %all-to-all-start.12 = ((bf16[64,2,128]{2,1,0:T(2,128)(2,1)}), bf16[64,2,128]{2,1,0:T(2,128)(2,1)S(1)}, u32[]{:S(2)}, u32[]{:S(2)}) async-start(bf16[64,2,128]{2,1,0:T(2,128)(2,1)} %reshape.2282), calls=%async_computation.12 | async-start | bytes 65536 | tf_op jit(solution)/shard_map/all_to_all | solution.py:92
  363.1 16.1 %all-to-all-start.13 = ((bf16[64,2,128]{2,1,0:T(2,128)(2,1)}), bf16[64,2,128]{2,1,0:T(2,128)(2,1)S(1)}, u32[]{:S(2)}, u32[]{:S(2)}) async-start(bf16[64,2,128]{2,1,0:T(2,128)(2,1)} %reshape.2288), calls=%async_computation.13 | async-start | bytes 65536 | tf_op jit(solution)/shard_map/all_to_all | solution.py:92
  386.1 83.7 %all-to-all-start.14 = ((bf16[64,2,128]{2,1,0:T(2,128)(2,1)}), bf16[64,2,128]{2,1,0:T(2,128)(2,1)S(1)}, u32[]{:S(2)}, u32[]{:S(2)}) async-start(bf16[64,2,128]{2,1,0:T(2,128)(2,1)} %reshape.2292), calls=%async_computation.14 | async-start | bytes 65536 | tf_op jit(solution)/shard_map/all_to_all | solution.py:91
  390.8 323.1 %all-reduce.4.cloned.1.call-start = ((), (), s32[]{:S(2)}) async-start(), calls=%async_computation.18 | async-start | bytes 540672 | tf_op jit(solution)/shard_map/psum | solution.py:152
  494.4 221.8 %all-to-all-start.15 = ((bf16[64,2,128]{2,1,0:T(2,128)(2,1)}), bf16[64,2,128]{2,1,0:T(2,128)(2,1)S(1)}, u32[]{:S(2)}, u32[]{:S(2)}) async-start(bf16[64,2,128]{2,1,0:T(2,128)(2,1)} %reshape.2294), calls=%async_computation.15 | async-start | bytes 65536 | tf_op jit(solution)/shard_map/all_to_all | solution.py:91
  713.9 1.6 copy-start.4
  716.1 16.1 %all-to-all-start.16 = ((bf16[64,2,128]{2,1,0:T(2,128)(2,1)}), bf16[64,2,128]{2,1,0:T(2,128)(2,1)S(1)}, u32[]{:S(2)}, u32[]{:S(2)}) async-start(bf16[64,2,128]{2,1,0:T(2,128)(2,1)} %reshape.2290), calls=%async_computation.16 | async-start | bytes 65536 | tf_op jit(solution)/shard_map/all_to_all | solution.py:92
  750.8 16.1 %all-to-all-start.17 = ((bf16[64,2,128]{2,1,0:T(2,128)(2,1)}), bf16[64,2,128]{2,1,0:T(2,128)(2,1)S(1)}, u32[]{:S(2)}, u32[]{:S(2)}) async-start(bf16[64,2,128]{2,1,0:T(2,128)(2,1)} %reshape.2296), calls=%async_computation.17 | async-start | bytes 65536 | tf_op jit(solution)/shard_map/all_to_all | solution.py:92
Sparse Core Ops, SparseCore 0:
  469.9 243.8 all-reduce.3
where the time goes:
time: 787 us; the launch traced here: 777 us
  waiting for transfers between devices  293 us (37%)
  other arithmetic  165 us (21%)
  starting transfers between devices  129 us (16%)
  local copies, waits for them, and re-layouts  91.6 us (12%)
  blocking collectives  77.8 us (10%)
  between operations  16.9 us (2%)
    psum x1, waiting for transfers between devices, body(): lax.psum((part_wru, part_bru, cand_sums[0], cand_sums[1]), ('snap', 'dom'))  212 us
    scatter-add x36, other arithmetic, spread(): total.at[:, :, index[slot]].add(values.astype(jnp.float32) * weights[slot])  121 us
    psum x1, blocking collectives, body(): lax.psum((part_wru, part_bru, cand_sums[0], cand_sums[1]), ('snap', 'dom'))  77.8 us
    all_to_all x11, starting transfers between devices, body(): lax.all_to_all(buffer, 'dom', split_axis=2, concat_axis=2, tiled=True)  77.5 us
    all_to_all x6, starting transfers between devices, body(): lax.all_to_all(buffer.astype(jnp.bfloat16), 'dom', split_axis=2, concat_a...  46.8 us
    gather x56, local copies, waits for them, and re-layouts, collect(): jnp.take(extended, index[slot], axis=2).astype(jnp.float32) * weights[slot]  45.2 us
    all_to_all x11, waiting for transfers between devices, body(): lax.all_to_all(buffer, 'dom', split_axis=2, concat_axis=2, tiled=True)  39.9 us
    all_to_all x6, waiting for transfers between devices, body(): lax.all_to_all(buffer.astype(jnp.bfloat16), 'dom', split_axis=2, concat_a...  34.1 us
  transfers between devices with their start and end apart: 19, of which 14 were waited for; matrix products, arithmetic and copies ran while one was open for 14% of the time, Pallas kernels for 0%

commit v1 on v0

v1 whole, which is shorter than its diff:
```python
import math

import jax
import jax.numpy as jnp
from jax import lax
from jax.experimental import pallas as pl
from jax.experimental.pallas import tpu as pltpu
from jax.sharding import PartitionSpec as P

F32, BF16 = jnp.float32, jnp.bfloat16
MESH = pl.DeviceIdType.MESH
HOPS = 8


def mm(a, b):
    return jnp.dot(a, b, preferred_element_type=F32)


def turn(a):
    return jnp.transpose(a.astype(F32))


def lanes(rows, width):
    return lax.broadcasted_iota(jnp.int32, (rows, width), 1)


def forward_map(lane, chans, fin):
    tile, at = lane // 128, lane % 128
    upper, low = at >= 64, at % 64
    first = jnp.where(upper, 3 * chans, chans) + fin + low
    second = jnp.where(upper, 4 * chans, 2 * chans) + fin + low
    third = jnp.where(upper, jnp.where(low < fin, low, -1), fin + low)
    order = jnp.where(upper, 3, 1) + low // fin
    fourth = jnp.where(low < 2 * fin, order * chans + low % fin, -1)
    return jnp.where(tile == 0, first, jnp.where(tile == 1, second, jnp.where(tile == 2, third, fourth)))


def backward_map(lane, chans, fin):
    tile, at = lane // 128, lane % 128
    upper, low = at >= 64, at % 64
    order = jnp.where(
        tile == 0, jnp.where(upper, 2, 4), jnp.where(tile == 1, jnp.where(upper, 1, 3), 0)
    )
    return order * chans + fin + low


def kernel(
    n_dom, width, fin, chans, halo,
    readings_ref, previous_ref, upstream_ref, gw_ref, gb_ref, cw_ref, cb_ref, nb_ref, ew_ref, sr_ref,
    state_ref, pg_ref,
    sp, ml, wl, sw, held, upward, scale_f, scale_a, local, wide, states, mixed, field, wg, wc, bg, bc,
    send_w, recv_w, send_n, recv_n, ssem, rsem, osem, rows,
):
    me = lax.axis_index("dom")
    barrier = pltpu.get_barrier_semaphore()

    def peer_of(k):
        return (me + k) % n_dom

    def greet(k, c):
        pl.semaphore_signal(barrier, inc=1, device_id={"dom": peer_of(k)}, device_id_type=MESH)
        return c

    lax.fori_loop(1, n_dom, greet, 0)

    lane128 = lanes(width, 128)
    low128 = lane128 < 64

    prev = previous_ref[0].astype(F32)
    held[...] = jnp.transpose(jnp.concatenate([prev, prev], axis=0))
    ups = upstream_ref[0].astype(F32)
    upward[...] = jnp.transpose(jnp.concatenate([ups, ups], axis=0))
    read = readings_ref[0].astype(F32)
    degs = nb_ref.shape[0]
    rows[...] = jnp.zeros_like(rows)
    rows[0, 0:fin, :] = read
    rows[0, 64 : 64 + fin, :] = read
    rows[1, 0:degs, :] = nb_ref[...].astype(F32)
    rows[1, 8 : 8 + degs, :] = ew_ref[...]
    rows[1, 16:17, :halo] = sr_ref[...].astype(F32)
    extra = jnp.transpose(rows[0])
    columns = jnp.transpose(rows[1])

    rows_sel = columns[:halo, 16:17].astype(jnp.int32)
    sp[:halo, :] = jnp.where(lanes(halo, width) == rows_sel, 1.0, 0.0).astype(BF16)

    def push_block(first, rows):
        here = lax.broadcasted_iota(jnp.int32, (rows, width), 0) + first
        total = jnp.zeros((rows, width), F32)
        for d in range(degs):
            total = total + jnp.where(nb_ref[d : d + 1, :] == here, ew_ref[d : d + 1, :], 0.0)
        return total

    edge_sums = push_block(width, halo)
    sp[halo:, :] = edge_sums.astype(BF16)
    deg_halo = jnp.sum(edge_sums, axis=1, keepdims=True)
    deg_high = deg_halo.astype(BF16).astype(F32)
    deg_rest = deg_halo - deg_high

    def send_buf(hop):
        return send_w.at[hop] if hop < 2 else send_n.at[hop - 2]

    def recv_buf(hop):
        return recv_w.at[hop] if hop < 2 else recv_n.at[hop - 2]

    def launch(hop, values):
        span = values.shape[1]
        mixed_rows = mm(sp[...], values)
        out = jnp.where(
            lanes(halo, span) % 128 < 64, mixed_rows[halo:, :], mixed_rows[:halo, :]
        )
        if hop == 0:
            lane = lanes(halo, span)
            out = jnp.where(lane == 128 + fin, deg_high, jnp.where(lane == 128 + fin + 1, deg_rest, out))
        out = out.astype(BF16)
        src, dst = send_buf(hop), recv_buf(hop)
        for part in range(span // 128):
            src.at[part].reshape(halo, 128)[...] = out[:, part * 128 : part * 128 + 128]

        if hop == 0:
            pl.semaphore_wait(barrier, n_dom - 1)

        def go(k, c):
            pltpu.make_async_remote_copy(
                src.at[:, peer_of(k)], dst.at[:, me], ssem.at[hop], rsem.at[hop],
                device_id={"dom": peer_of(k)}, device_id_type=MESH,
            ).start()
            return c

        lax.fori_loop(1, n_dom, go, 0)
        pltpu.make_async_copy(src.at[:, me], dst.at[:, me], osem.at[hop]).start()

    def near(values):
        span = values.shape[1]
        low = lanes(width, span) % 128 < 64
        return jnp.where(low, mm(ml[...], values), mm(wl[...], values))

    def await_recv(hop):
        src, dst = send_buf(hop), recv_buf(hop)
        pltpu.make_async_copy(
            src.at[:, pl.ds(0, n_dom - 1)], dst.at[:, pl.ds(0, n_dom - 1)], rsem.at[hop]
        ).wait()
        pltpu.make_async_copy(src.at[:, me], dst.at[:, me], osem.at[hop]).wait()

    def far(hop):
        dst = recv_buf(hop)
        span = 256 if hop < 2 else 128
        got = [dst.at[part].reshape(halo, 128)[...] for part in range(span // 128)]
        got = got[0] if len(got) == 1 else jnp.concatenate(got, axis=1)
        both = mm(sw[...], got)
        low = lanes(width, span) % 128 < 64
        return jnp.where(low, both[:width, :], both[width:, :])

    start = jnp.concatenate([held[...], extra], axis=1)
    launch(0, start.astype(BF16))

    wts = [columns[:, 8 + d : 9 + d] for d in range(degs)]
    srcs = [columns[:, d : d + 1].astype(jnp.int32) for d in range(degs)]
    for first in range(0, width, 128):
        here = lanes(128, width + halo)
        total = jnp.zeros((128, width + halo), F32)
        for d in range(degs):
            total = total + jnp.where(srcs[d][first : first + 128] == here, wts[d][first : first + 128], 0.0)
        total = total.astype(BF16)
        wl[first : first + 128, :] = total[:, :width]
        sw[width + first : width + first + 128, :] = total[:, width:]
    deg_near = []
    for first in range(0, width, 128):
        block = push_block(first, 128)
        ml[first : first + 128, :] = block.astype(BF16)
        deg_near.append(jnp.sum(block, axis=1, keepdims=True))
    deg_near = jnp.concatenate(deg_near, axis=0)
    sw[:width, :] = jnp.where(
        lax.broadcasted_iota(jnp.int32, (width, halo), 0) == sr_ref[...], 1.0, 0.0
    ).astype(BF16)
    deg_in = wts[0]
    for d in range(1, degs):
        deg_in = deg_in + wts[d]
    inv_in = 1.0 / deg_in

    cols = gw_ref.shape[1]
    pick = (
        lax.broadcasted_iota(jnp.int32, (cols, 512), 0) == forward_map(lanes(1, 512), chans, fin)
    )
    pick = jnp.where(pick, 1.0, 0.0).astype(BF16)
    pick_b = (
        lax.broadcasted_iota(jnp.int32, (cols, 384), 0) == backward_map(lanes(1, 384), chans, fin)
    )
    pick_b = jnp.where(pick_b, 1.0, 0.0).astype(BF16)
    gate_w = gw_ref[...]
    cand_w = cw_ref[...]
    gate_f = mm(gate_w, pick)
    cand_f = mm(cand_w, pick)
    r, u = gate_f[:64], gate_f[64:]
    wg[...] = jnp.transpose(jnp.concatenate([r, r, u, u], axis=0)).astype(BF16)
    wc[...] = jnp.transpose(jnp.concatenate([cand_f, cand_f], axis=0)).astype(BF16)
    bg[...] = mm(gate_w, pick_b).astype(BF16)
    bc[:64, :] = mm(cand_w, pick_b).astype(BF16)
    bc[64:, :] = jnp.zeros((64, 384), BF16)

    wide[...] = near(start.astype(BF16))
    await_recv(0)
    raw = far(0)
    deg_out = deg_near + raw[:, 128 + fin : 129 + fin] + raw[:, 129 + fin : 130 + fin]
    raw = raw + wide[...]
    inv_out = 1.0 / deg_out
    scale_f[...] = jnp.where(low128, inv_out, inv_in)
    scale_a[...] = jnp.where(low128, inv_in, inv_out)
    first_main = (raw[:, :128] * scale_f[...]).astype(BF16)
    states[:, :128] = first_main
    first_extra = jnp.where(lane128 % 64 < fin, raw[:, 128:] * scale_f[...], 0.0)
    second_in = jnp.concatenate([first_main, first_extra.astype(BF16)], axis=1)
    launch(1, second_in)
    ones = jnp.where(
        low128, held[...], jnp.where(lane128 < 64 + fin, extra, jnp.where(lane128 == 64 + fin, 1.0, 0.0))
    )
    states[:, 256:384] = ones.astype(BF16)
    wide[...] = near(second_in)
    await_recv(1)
    raw = far(1) + wide[...]
    states[:, 128:256] = (2.0 * raw[:, :128] * scale_f[...] - held[...]).astype(BF16)
    second_extra = 2.0 * raw[:, 128:] * scale_f[...] - extra
    tail = first_extra.astype(BF16).astype(F32) + pltpu.roll(second_extra.astype(BF16).astype(F32), fin, 1)
    states[:, 384:] = tail.astype(BF16)

    gates = mm(states[...], wg[...])
    bias = jnp.broadcast_to(gb_ref[...], (width, 128))
    turned = pltpu.roll(bias, 64, 1)
    reset = jax.nn.sigmoid(gates[:, :128] + jnp.where(low128, bias, turned))
    update = jax.nn.sigmoid(gates[:, 128:] + jnp.where(low128, turned, bias))
    scaled = (reset * held[...]).astype(BF16)

    launch(2, scaled)
    mixed[:, 256:384] = jnp.where(low128, scaled, states[:, 256:384])
    mixed[:, 384:] = states[:, 384:]
    local[...] = near(scaled)
    await_recv(2)
    hop_one = ((far(2) + local[...]) * scale_f[...]).astype(BF16)
    launch(3, hop_one)
    mixed[:, :128] = hop_one
    local[...] = near(hop_one)
    await_recv(3)
    raw = far(3) + local[...]
    mixed[:, 128:256] = (2.0 * raw * scale_f[...] - scaled.astype(F32)).astype(BF16)
    cand = jnp.tanh(mm(mixed[...], wc[...]) + cb_ref[...])
    cand_grad = (upward[...] * (1.0 - update) * (1.0 - cand * cand)).astype(BF16)

    def back(grad, weights, hop):
        outer = mm(grad, weights[:, :128])
        values = (outer * scale_a[...]).astype(BF16)
        launch(hop, values)
        local[...] = near(values)
        inner = mm(grad, weights[:, 128:256])
        direct = mm(grad, weights[:, 256:384]) - outer - pltpu.roll(outer, 64, 1)
        field[...] = direct
        await_recv(hop)
        raw = far(hop) + local[...]
        values = ((inner + 2.0 * raw) * scale_a[...]).astype(BF16)
        launch(hop + 1, values)
        local[...] = near(values)
        return values

    def back_end(hop):
        await_recv(hop + 1)
        raw = far(hop + 1) + local[...]
        return field[...] + raw + pltpu.roll(raw, 64, 1)

    back(cand_grad, bc, 4)
    pg_ref[128:, :] = mm(turn(cand_grad)[:64, :].astype(BF16), mixed[...])
    scaled_grad = back_end(4)
    reset_part = scaled_grad * held[...] * reset * (1.0 - reset)
    update_part = upward[...] * (held[...] - cand) * update * (1.0 - update)
    gate_grad = jnp.where(low128, reset_part, update_part).astype(BF16)
    back(gate_grad, bg, 6)
    pg_ref[:128, :] = mm(turn(gate_grad).astype(BF16), states[...])
    state_part = back_end(6)
    result = upward[...] * update + scaled_grad * reset + state_part
    state_ref[0] = jnp.transpose(result)[:64, :].astype(BF16)

    for hop in range(HOPS):
        src, dst = send_buf(hop), recv_buf(hop)
        pltpu.make_async_copy(
            src.at[:, pl.ds(0, n_dom - 1)], dst.at[:, pl.ds(0, n_dom - 1)], ssem.at[hop]
        ).wait()


def unpermute(grads, chans, fin):
    starts = {1: 0, 3: 64, 2: 128, 4: 192, 0: 256}
    reads = {0: 320, 1: 384, 2: 384 + fin, 3: 448, 4: 448 + fin}
    parts = []
    for m in range(5):
        parts.append(grads[:, reads[m] : reads[m] + fin])
        parts.append(grads[:, starts[m] : starts[m] + chans - fin])
    return jnp.concatenate(parts, axis=1), grads[:, 320 + fin]


def solution(mesh):
    n_dom = mesh.shape["dom"]

    def body(readings, previous, upstream, gw, gb, cw, cb, nb, ew, sr):
        fin, hidden, width = readings.shape[1], previous.shape[1], readings.shape[2]
        chans, halo = fin + hidden, sr.shape[1]
        slots = halo // n_dom
        vmem = pl.BlockSpec(memory_space=pltpu.VMEM)

        def run(*refs):
            kernel(n_dom, width, fin, chans, halo, *refs)

        state, grads = pl.pallas_call(
            run,
            out_shape=(
                jax.ShapeDtypeStruct((1, hidden, width), BF16),
                jax.ShapeDtypeStruct((192, 512), F32),
            ),
            in_specs=[vmem] * 10,
            out_specs=(vmem, vmem),
            scratch_shapes=[
                pltpu.VMEM((2 * halo, width), BF16),
                pltpu.VMEM((width, width), BF16),
                pltpu.VMEM((width, width), BF16),
                pltpu.VMEM((2 * width, halo), BF16),
                pltpu.VMEM((width, 128), F32),
                pltpu.VMEM((width, 128), F32),
                pltpu.VMEM((width, 128), F32),
                pltpu.VMEM((width, 128), F32),
                pltpu.VMEM((width, 128), F32),
                pltpu.VMEM((width, 256), F32),
                pltpu.VMEM((width, 512), BF16),
                pltpu.VMEM((width, 512), BF16),
                pltpu.VMEM((width, 128), F32),
                pltpu.VMEM((512, 256), BF16),
                pltpu.VMEM((512, 128), BF16),
                pltpu.VMEM((128, 384), BF16),
                pltpu.VMEM((128, 384), BF16),
                pltpu.VMEM((2, 2, n_dom, slots, 128), BF16),
                pltpu.VMEM((2, 2, n_dom, slots, 128), BF16),
                pltpu.VMEM((HOPS - 2, 1, n_dom, slots, 128), BF16),
                pltpu.VMEM((HOPS - 2, 1, n_dom, slots, 128), BF16),
                pltpu.SemaphoreType.DMA((HOPS,)),
                pltpu.SemaphoreType.DMA((HOPS,)),
                pltpu.SemaphoreType.DMA((HOPS,)),
                pltpu.VMEM((2, 128, width), F32),
            ],
            compiler_params=pltpu.CompilerParams(collective_id=0, has_side_effects=True),
        )(readings, previous, upstream, gw, gb.reshape(1, -1), cw, jnp.tile(cb.reshape(1, -1), (1, 2)), nb, ew, sr)
        factor = 1.0 / math.sqrt(readings.shape[0] * lax.axis_size("snap") * width * n_dom)
        grads = lax.psum(grads, ("snap", "dom")) * factor
        all_w, all_b = unpermute(grads, chans, fin)
        return state, all_w[:128], all_b[:128], all_w[128:], all_b[128:]

    in_specs = (
        P("snap", None, "dom"), P("snap", None, "dom"), P("snap", None, "dom"),
        P(), P(), P(), P(), P(None, "dom"), P(None, "dom"), P("dom", None),
    )
    out_specs = (P("snap", None, "dom"), P(), P(), P(), P())
    return jax.shard_map(body, mesh=mesh, in_specs=in_specs, out_specs=out_specs, check_vma=False)
```

time: 787 us -> 343 us (0.44); the launches traced: 777 us -> 342 us
  other arithmetic: 165 us -> 1.03 us
  starting transfers between devices: 129 us -> 0.04 us
  local copies, waits for them, and re-layouts: 91.6 us -> 7 us
  blocking collectives: 77.8 us -> 0 us
  Pallas kernels: 0 us -> 71.6 us
  waiting for transfers between devices: 293 us -> 249 us
    scatter-add x45 -> x0, other arithmetic: 140 us -> none  [the longest x36 121 us: spread(): total.at[:, :, index[slot]].add(values.astype(jnp.float32) * weights[slot])]
    all_to_all x18 -> x0, starting transfers between devices: 129 us -> none  [the longest x11 77.5 us: body(): lax.all_to_all(buffer, 'dom', split_axis=2, concat_axis=2, tiled=True)]
    all_to_all x18 -> x0, waiting for transfers between devices: 81.7 us -> none  [the longest x11 39.9 us: body(): lax.all_to_all(buffer, 'dom', split_axis=2, concat_axis=2, tiled=True)]
    psum x1 -> x0, blocking collectives: 77.8 us -> none  [body(): lax.psum((part_wru, part_bru, cand_sums[0], cand_sums[1]), ('snap', 'dom'))]
    pallas_call x0 -> x1, Pallas kernels: none -> 71.6 us  [body(): pl.pallas_call(run, out_shape=(jax.ShapeDtypeStruct((1, hidden, width), B...]
    gather x67 -> x0, local copies, waits for them, and re-layouts: 62.6 us -> none  [the longest x56 45.2 us: collect(): jnp.take(extended, index[slot], axis=2).astype(jnp.float32) * weights[slot]]
    psum x1, waiting for transfers between devices: 212 us -> 249 us  [body(): grads = lax.psum(grads, ('snap', 'dom')) * factor]
    unnamed x17 -> x0, other arithmetic: 15.1 us -> none
  transfers between devices with their start and end apart: 19 -> 1, of which waited for: 14 -> 1; matrix products, arithmetic and copies ran while one was open for 14% -> 0% of each run, Pallas kernels for 0% -> 0%
where the time goes in v1:
time: 343 us; the launch traced here: 342 us
  waiting for transfers between devices  249 us (73%)
  Pallas kernels  71.6 us (21%)
  between operations  14.1 us (4%)
  local copies, waits for them, and re-layouts  7 us (2%)
    psum x1, waiting for transfers between devices, body(): grads = lax.psum(grads, ('snap', 'dom')) * factor  249 us
    pallas_call x1, Pallas kernels, body(): pl.pallas_call(run, out_shape=(jax.ShapeDtypeStruct((1, hidden, width), B...  71.6 us
  transfers between devices with their start and end apart: 1, of which 1 were waited for; matrix products, arithmetic and copies ran while one was open for 0% of the time, Pallas kernels for 0%

profile of v1, /device:TPU:1, one launch (start us, length us, event | category | flops | bytes accessed | tf_op | source)
XLA Modules:
  0.0 342.5 jit_solution(2293949246457183833)
XLA Ops:
  7.2 0.0 all-reduce.2.cloned.1.call-start
  7.2 0.7 tile.8
  7.9 0.6 tile.9.refs_6_
  8.5 1.6 copy.17.refs_3_
  10.1 71.6 %shard_map.137 = (bf16[1,64,512]{2,1,0:T(8,128)(2,1)}, f32[192,512]{1,0:T(8,128)}) custom-call(bf16[1,2,512]{2,1,0:T(2,128)(2,1)} %refs_0_.1, bf16[1,64,512]{2,1,0:T(8,128)(2,1)} %refs_1_.1, bf16[1,64,512]{2,1,0:T(8,128)(2,1)} %refs_2_.1, bf16[128,330]{1,0:T(8,128)(2,1)} %copy.17.refs_3_, f32[1,128]{1,0:T(1,128)} %bitcast.1, bf16[64,330]{1,0:T(8,128)(2,1)} %refs_5_.1, ...), custom_call_target="tpu_custom_call" | custom-call | tf_op jit(solution)/shard_map/pallas_call | solution.py:309
  81.7 0.0 all-reduce.2.cloned.1.call-update
  81.7 248.7 %all-reduce.2.cloned.1.call-done = f32[192,512]{1,0:T(8,128)} async-done(((f32[192,512]{1,0:T(8,128)}), f32[192,512]{1,0:T(8,128)}) %all-reduce.2.cloned.1.call-update) | async-done | bytes 393232 | tf_op jit(solution)/shard_map/psum | solution.py:347
  330.4 1.0 broadcast_multiply_fusion
  331.5 0.7 slice_reduce_fusion.1
  332.2 0.7 slice_reduce_fusion
  332.9 0.1 fusion
  333.0 0.2 fusion.1
  333.1 0.3 concatenate.3
  333.5 0.7 slice.79
  334.2 0.0 copy-start
  334.2 0.8 copy.18
  335.0 0.0 copy-done
  335.0 0.6 copy.21
  (1 shorter events, 0.0 us)
Async XLA Ops:
  7.2 323.3 %all-reduce.2.cloned.1.call-start = ((), (), s32[]{:S(2)}) async-start(), calls=%async_computation | async-start | bytes 786432 | tf_op jit(solution)/shard_map/psum | solution.py:347
  334.2 0.8 copy-start
Sparse Core Ops, SparseCore 0:
  81.9 248.5 all-reduce.1

commit v2 on v1

--- a/solution.py
+++ b/solution.py
@@ -10,6 +10,7 @@
 F32, BF16 = jnp.float32, jnp.bfloat16
 MESH = pl.DeviceIdType.MESH
 HOPS = 8
+RS_EARLY, AG_EARLY, RS_LATE, AG_LATE, GROUPS = 8, 9, 10, 11, 12
 
 
 def mm(a, b):
@@ -45,11 +46,12 @@
 
 
 def kernel(
-    n_dom, width, fin, chans, halo,
+    n_dom, n_snap, width, fin, chans, halo, factor,
     readings_ref, previous_ref, upstream_ref, gw_ref, gb_ref, cw_ref, cb_ref, nb_ref, ew_ref, sr_ref,
-    state_ref, pg_ref,
+    state_ref, gate_out, gate_bias_out, cand_out, cand_bias_out,
     sp, ml, wl, sw, held, upward, scale_f, scale_a, local, wide, states, mixed, field, wg, wc, bg, bc,
     send_w, recv_w, send_n, recv_n, ssem, rsem, osem, rows,
+    early, late, piece_e, piece_l, snap_send, snap_recv, snap_s, snap_r, back_pick,
 ):
     me = lax.axis_index("dom")
     barrier = pltpu.get_barrier_semaphore()
@@ -62,6 +64,9 @@
         return c
 
     lax.fori_loop(1, n_dom, greet, 0)
+    mine = lax.axis_index("snap")
+    for k in range(1, n_snap):
+        pl.semaphore_signal(barrier, inc=1, device_id={"snap": (mine + k) % n_snap}, device_id_type=MESH)
 
     lane128 = lanes(width, 128)
     low128 = lane128 < 64
@@ -98,10 +103,40 @@
     deg_rest = deg_halo - deg_high
 
     def send_buf(hop):
+        if hop >= HOPS:
+            return {RS_EARLY: early.at[0], RS_LATE: late.at[0]}[hop]
         return send_w.at[hop] if hop < 2 else send_n.at[hop - 2]
 
     def recv_buf(hop):
+        if hop >= HOPS:
+            return {RS_EARLY: early.at[1], AG_EARLY: early.at[2], RS_LATE: late.at[1], AG_LATE: late.at[2]}[hop]
         return recv_w.at[hop] if hop < 2 else recv_n.at[hop - 2]
+
+    def send_all(group):
+        src, dst = send_buf(group), recv_buf(group)
+
+        def go(k, c):
+            pltpu.make_async_remote_copy(
+                src.at[:, peer_of(k)], dst.at[:, me], ssem.at[group], rsem.at[group],
+                device_id={"dom": peer_of(k)}, device_id_type=MESH,
+            ).start()
+            return c
+
+        lax.fori_loop(1, n_dom, go, 0)
+        pltpu.make_async_copy(src.at[:, me], dst.at[:, me], osem.at[group]).start()
+
+    def spread_piece(group, src):
+        dst = recv_buf(group)
+
+        def go(k, c):
+            pltpu.make_async_remote_copy(
+                src, dst.at[:, me], ssem.at[group], rsem.at[group],
+                device_id={"dom": peer_of(k)}, device_id_type=MESH,
+            ).start()
+            return c
+
+        lax.fori_loop(1, n_dom, go, 0)
+        pltpu.make_async_copy(src, dst.at[:, me], osem.at[group]).start()
 
     def launch(hop, values):
         span = values.shape[1]
@@ -113,22 +148,13 @@
             lane = lanes(halo, span)
             out = jnp.where(lane == 128 + fin, deg_high, jnp.where(lane == 128 + fin + 1, deg_rest, out))
         out = out.astype(BF16)
-        src, dst = send_buf(hop), recv_buf(hop)
+        src = send_buf(hop)
         for part in range(span // 128):
             src.at[part].reshape(halo, 128)[...] = out[:, part * 128 : part * 128 + 128]
 
         if hop == 0:
-            pl.semaphore_wait(barrier, n_dom - 1)
-
-        def go(k, c):
-            pltpu.make_async_remote_copy(
-                src.at[:, peer_of(k)], dst.at[:, me], ssem.at[hop], rsem.at[hop],
-                device_id={"dom": peer_of(k)}, device_id_type=MESH,
-            ).start()
-            return c
-
-        lax.fori_loop(1, n_dom, go, 0)
-        pltpu.make_async_copy(src.at[:, me], dst.at[:, me], osem.at[hop]).start()
+            pl.semaphore_wait(barrier, n_dom + n_snap - 2)
+        send_all(hop)
 
     def near(values):
         span = values.shape[1]
@@ -136,11 +162,46 @@
         return jnp.where(low, mm(ml[...], values), mm(wl[...], values))
 
     def await_recv(hop):
-        src, dst = send_buf(hop), recv_buf(hop)
-        pltpu.make_async_copy(
-            src.at[:, pl.ds(0, n_dom - 1)], dst.at[:, pl.ds(0, n_dom - 1)], rsem.at[hop]
-        ).wait()
-        pltpu.make_async_copy(src.at[:, me], dst.at[:, me], osem.at[hop]).wait()
+        dst = recv_buf(hop)
+        rest = dst.at[:, pl.ds(0, n_dom - 1)]
+        pltpu.make_async_copy(rest, rest, rsem.at[hop]).wait()
+        pltpu.make_async_copy(dst.at[:, me], dst.at[:, me], osem.at[hop]).wait()
+
+    def reduce_pieces(group, which):
+        await_recv(group)
+        dst = recv_buf(group)
+        parts = dst.shape[0]
+        row = lax.broadcasted_iota(jnp.int32, (8, halo * parts), 0)
+        col = lanes(8, halo * parts)
+        slots = dst.shape[2]
+        chosen = (col % slots == row % slots) & (col // halo == (row // slots) % parts)
+        chosen = jnp.where(chosen, 1.0, 0.0).astype(BF16)
+        terms = [dst.at[part].reshape(halo, 128)[...] for part in range(parts)]
+        total = mm(chosen[:, :halo], terms[0])
+        for part in range(1, parts):
+            total = total + mm(chosen[:, part * halo : part * halo + halo], terms[part])
+        snap_send[which] = total
+        snap_recv[which, mine] = total
+        for k in range(1, n_snap):
+            pltpu.make_async_remote_copy(
+                snap_send.at[which], snap_recv.at[which, mine], snap_s.at[which], snap_r.at[which],
+                device_id={"snap": (mine + k) % n_snap}, device_id_type=MESH,
+            ).start()
+
+    def finish_pieces(group, which, piece):
+        others = snap_recv.at[which, pl.ds(0, n_snap - 1)]
+        pltpu.make_async_copy(others, others, snap_r.at[which]).wait()
+        total = snap_recv[which, 0]
+        for k in range(1, n_snap):
+            total = total + snap_recv[which, k]
+        slots = piece.shape[1]
+        for part in range(piece.shape[0]):
+            piece[part] = total[part * slots : (part + 1) * slots, :].astype(BF16)
+        spread_piece(group, piece)
+
+    def gathered(group, tile, count):
+        at = tile * count
+        return recv_buf(group).at[at // halo].reshape(halo, 128)[at % halo : at % halo + count, :]
 
     def far(hop):
         dst = recv_buf(hop)
@@ -187,6 +248,10 @@
         lax.broadcasted_iota(jnp.int32, (cols, 384), 0) == backward_map(lanes(1, 384), chans, fin)
     )
     pick_b = jnp.where(pick_b, 1.0, 0.0).astype(BF16)
+    column = lax.broadcasted_iota(jnp.int32, (512, 1), 0)
+    back_pick[...] = jnp.where(
+        lanes(512, 384) == forward_map(column, chans, fin), 1.0, 0.0
+    ).astype(BF16)
     gate_w = gw_ref[...]
     cand_w = cw_ref[...]
     gate_f = mm(gate_w, pick)
@@ -245,57 +310,92 @@
     cand = jnp.tanh(mm(mixed[...], wc[...]) + cb_ref[...])
     cand_grad = (upward[...] * (1.0 - update) * (1.0 - cand * cand)).astype(BF16)
 
-    def back(grad, weights, hop):
+    update_part = upward[...] * (held[...] - cand) * update * (1.0 - update)
+
+    def outer_hop(grad, weights, hop):
         outer = mm(grad, weights[:, :128])
         values = (outer * scale_a[...]).astype(BF16)
         launch(hop, values)
+        return outer, values
+
+    def inner_hop(grad, weights, hop, outer, values, meanwhile):
         local[...] = near(values)
         inner = mm(grad, weights[:, 128:256])
-        direct = mm(grad, weights[:, 256:384]) - outer - pltpu.roll(outer, 64, 1)
-        field[...] = direct
+        field[...] = mm(grad, weights[:, 256:384]) - outer - pltpu.roll(outer, 64, 1)
+        meanwhile()
         await_recv(hop)
         raw = far(hop) + local[...]
         values = ((inner + 2.0 * raw) * scale_a[...]).astype(BF16)
         launch(hop + 1, values)
         local[...] = near(values)
-        return values
-
-    def back_end(hop):
-        await_recv(hop + 1)
-        raw = far(hop + 1) + local[...]
+
+    def last_hop(hop):
+        await_recv(hop)
+        raw = far(hop) + local[...]
         return field[...] + raw + pltpu.roll(raw, 64, 1)
 
-    back(cand_grad, bc, 4)
-    pg_ref[128:, :] = mm(turn(cand_grad)[:64, :].astype(BF16), mixed[...])
-    scaled_grad = back_end(4)
+    def early_sums():
+        grads = turn(jnp.where(low128, cand_grad.astype(F32), update_part)).astype(BF16)
+        by_cand = mm(grads[:64, :], mixed[...])
+        by_update = mm(grads[64:, :], states[...])
+        for tile in range(4):
+            dst = early.at[0, tile // 2].reshape(halo, 128)
+            at = tile % 2 * 128
+            dst[at : at + 64, :] = by_cand[:, tile * 128 : tile * 128 + 128].astype(BF16)
+            dst[at + 64 : at + 128, :] = by_update[:, tile * 128 : tile * 128 + 128].astype(BF16)
+        send_all(RS_EARLY)
+
+    outer, values = outer_hop(cand_grad, bc, 4)
+    inner_hop(cand_grad, bc, 4, outer, values, early_sums)
+    reduce_pieces(RS_EARLY, 0)
+    scaled_grad = last_hop(5)
     reset_part = scaled_grad * held[...] * reset * (1.0 - reset)
-    update_part = upward[...] * (held[...] - cand) * update * (1.0 - update)
     gate_grad = jnp.where(low128, reset_part, update_part).astype(BF16)
-    back(gate_grad, bg, 6)
-    pg_ref[:128, :] = mm(turn(gate_grad).astype(BF16), states[...])
-    state_part = back_end(6)
+    outer, values = outer_hop(gate_grad, bg, 6)
+    by_reset = mm(turn(gate_grad)[:64, :].astype(BF16), states[...])
+    for tile in range(4):
+        late.at[0, 0].reshape(halo, 128)[tile * 64 : tile * 64 + 64, :] = by_reset[
+            :, tile * 128 : tile * 128 + 128
+        ].astype(BF16)
+    send_all(RS_LATE)
+    inner_hop(gate_grad, bg, 6, outer, values, lambda: finish_pieces(AG_EARLY, 0, piece_e))
+    reduce_pieces(RS_LATE, 1)
+    finish_pieces(AG_LATE, 1, piece_l)
+
+    await_recv(AG_EARLY)
+    bias_row = jnp.where(lanes(8, 128) == 64 + fin, 1.0, 0.0).astype(BF16)
+
+    def put(tiles, weight_out, bias_out):
+        total = mm(tiles[0], back_pick[:128, :])
+        for tile in range(1, 4):
+            total = total + mm(tiles[tile], back_pick[tile * 128 : tile * 128 + 128, :])
+        weight_out[...] = total[:, : weight_out.shape[1]] * factor
+        bias = lax.dot_general(bias_row, tiles[2], (((1,), (1,)), ((), ())), preferred_element_type=F32)
+        bias_out[...] = bias[0:1, :] * factor
+
+    put([gathered(AG_EARLY, tile, 128)[:64] for tile in range(4)], cand_out, cand_bias_out)
+    state_part = last_hop(7)
     result = upward[...] * update + scaled_grad * reset + state_part
     state_ref[0] = jnp.transpose(result)[:64, :].astype(BF16)
-
-    for hop in range(HOPS):
-        src, dst = send_buf(hop), recv_buf(hop)
-        pltpu.make_async_copy(
-            src.at[:, pl.ds(0, n_dom - 1)], dst.at[:, pl.ds(0, n_dom - 1)], ssem.at[hop]
-        ).wait()
-
-
-def unpermute(grads, chans, fin):
-    starts = {1: 0, 3: 64, 2: 128, 4: 192, 0: 256}
-    reads = {0: 320, 1: 384, 2: 384 + fin, 3: 448, 4: 448 + fin}
-    parts = []
-    for m in range(5):
-        parts.append(grads[:, reads[m] : reads[m] + fin])
-        parts.append(grads[:, starts[m] : starts[m] + chans - fin])
-    return jnp.concatenate(parts, axis=1), grads[:, 320 + fin]
+    await_recv(AG_LATE)
+    put(
+        [
+            jnp.concatenate([gathered(AG_LATE, tile, 64), gathered(AG_EARLY, tile, 128)[64:]], axis=0)
+            for tile in range(4)
+        ],
+        gate_out, gate_bias_out,
+    )
+
+    for group in range(GROUPS):
+        rest = recv_buf(group).at[:, pl.ds(0, n_dom - 1)]
+        pltpu.make_async_copy(rest, rest, ssem.at[group]).wait()
+    for which in range(2):
+        others = snap_recv.at[which, pl.ds(0, n_snap - 1)]
+        pltpu.make_async_copy(others, others, snap_s.at[which]).wait()
 
 
 def solution(mesh):
-    n_dom = mesh.shape["dom"]
+    n_dom, n_snap = mesh.shape["dom"], mesh.shape["snap"]
 
     def body(readings, previous, upstream, gw, gb, cw, cb, nb, ew, sr):
         fin, hidden, width = readings.shape[1], previous.shape[1], readings.shape[2]
@@ -303,17 +403,23 @@
         slots = halo // n_dom
         vmem = pl.BlockSpec(memory_space=pltpu.VMEM)
 
+        factor = 1.0 / math.sqrt(readings.shape[0] * n_snap * width * n_dom)
+
         def run(*refs):
-            kernel(n_dom, width, fin, chans, halo, *refs)
-
-        state, grads = pl.pallas_call(
+            kernel(n_dom, n_snap, width, fin, chans, halo, factor, *refs)
+
+        cols = gw.shape[1]
+        state, gate, gate_b, cand, cand_b = pl.pallas_call(
             run,
             out_shape=(
                 jax.ShapeDtypeStruct((1, hidden, width), BF16),
-                jax.ShapeDtypeStruct((192, 512), F32),
+                jax.ShapeDtypeStruct((2 * hidden, cols), F32),
+                jax.ShapeDtypeStruct((1, 2 * hidden), F32),
+                jax.ShapeDtypeStruct((hidden, cols), F32),
+                jax.ShapeDtypeStruct((1, hidden), F32),
             ),
             in_specs=[vmem] * 10,
-            out_specs=(vmem, vmem),
+            out_specs=(vmem,) * 5,
             scratch_shapes=[
                 pltpu.VMEM((2 * halo, width), BF16),
                 pltpu.VMEM((width, width), BF16),
@@ -336,17 +442,23 @@
                 pltpu.VMEM((2, 2, n_dom, slots, 128), BF16),
                 pltpu.VMEM((HOPS - 2, 1, n_dom, slots, 128), BF16),
                 pltpu.VMEM((HOPS - 2, 1, n_dom, slots, 128), BF16),
-                pltpu.SemaphoreType.DMA((HOPS,)),
-                pltpu.SemaphoreType.DMA((HOPS,)),
-                pltpu.SemaphoreType.DMA((HOPS,)),
+                pltpu.SemaphoreType.DMA((GROUPS,)),
+                pltpu.SemaphoreType.DMA((GROUPS,)),
+                pltpu.SemaphoreType.DMA((GROUPS,)),
                 pltpu.VMEM((2, 128, width), F32),
+                pltpu.VMEM((3, 2, n_dom, slots, 128), BF16),
+                pltpu.VMEM((3, 1, n_dom, slots, 128), BF16),
+                pltpu.VMEM((2, slots, 128), BF16),
+                pltpu.VMEM((1, slots, 128), BF16),
+                pltpu.VMEM((2, 8, 128), F32),
+                pltpu.VMEM((2, n_snap, 8, 128), F32),
+                pltpu.SemaphoreType.DMA((2,)),
+                pltpu.SemaphoreType.DMA((2,)),
+                pltpu.VMEM((512, 384), BF16),
             ],
             compiler_params=pltpu.CompilerParams(collective_id=0, has_side_effects=True),
         )(readings, previous, upstream, gw, gb.reshape(1, -1), cw, jnp.tile(cb.reshape(1, -1), (1, 2)), nb, ew, sr)
-        factor = 1.0 / math.sqrt(readings.shape[0] * lax.axis_size("snap") * width * n_dom)
-        grads = lax.psum(grads, ("snap", "dom")) * factor
-        all_w, all_b = unpermute(grads, chans, fin)
-        return state, all_w[:128], all_b[:128], all_w[128:], all_b[128:]
+        return state, gate, gate_b.reshape(-1), cand, cand_b.reshape(-1)
 
     in_specs = (
         P("snap", None, "dom"), P("snap", None, "dom"), P("snap", None, "dom"),

time: 343 us -> 85.8 us (0.25)
  waiting for transfers between devices: 249 us -> 0 us
  between operations: 14.1 us -> 0.66 us
  Pallas kernels: 71.6 us -> 77.9 us
    psum x1 -> x0, waiting for transfers between devices: 249 us -> none  [body(): grads = lax.psum(grads, ('snap', 'dom')) * factor]
    pallas_call x1, Pallas kernels: 71.6 us -> 77.9 us  [body(): pl.pallas_call(run, out_shape=(jax.ShapeDtypeStruct((1, hidden, width), B...]
  transfers between devices with their start and end apart: 1 -> 0, of which waited for: 1 -> 0; matrix products, arithmetic and copies ran while one was open for 0% -> 0% of each run, Pallas kernels for 0% -> 0%
where the time goes in v2:
time: 85.8 us; the launch traced here: 85.6 us
  Pallas kernels  77.9 us (91%)
  local copies, waits for them, and re-layouts  6.99 us (8%)
    pallas_call x1, Pallas kernels, body(): pl.pallas_call(run, out_shape=(jax.ShapeDtypeStruct((1, hidden, width), B...  77.9 us
    unnamed x16, local copies, waits for them, and re-layouts  6.4 us

profile of v2, /device:TPU:1, one launch (start us, length us, event | category | flops | bytes accessed | tf_op | source)
XLA Modules:
  0.0 85.6 jit_solution(4792848786006953275)
XLA Ops:
  0.6 0.0 copy-start.2
  0.6 0.6 copy-done.2
  1.3 0.6 tile.9.refs_6_
  1.9 1.6 %copy.15.refs_3_ = bf16[128,330]{1,0:T(8,128)(2,1)} copy(bf16[128,330]{0,1:T(8,128)(2,1)} %param.13) | data formatting | bytes 168960 | tf_op args[3]
  3.5 77.9 %shard_map.137 = (bf16[1,64,512]{2,1,0:T(8,128)(2,1)}, f32[128,330]{1,0:T(8,128)}, f32[1,128]{1,0:T(1,128)}, f32[64,330]{1,0:T(8,128)}, f32[1,64]{1,0:T(1,128)}) custom-call(bf16[1,2,512]{2,1,0:T(2,128)(2,1)} %refs_0_.1, bf16[1,64,512]{2,1,0:T(8,128)(2,1)} %refs_1_.1, bf16[1,64,512]{2,1,0:T(8,128)(2,1)} %refs_2_.1, bf16[128,330]{1,0:T(8,128)(2,1)} %copy.15.refs_3_, ...), custom_call_target="tpu_custom_call" | custom-call | tf_op jit(solution)/shard_map/pallas_call | solution.py:412
  81.5 0.0 copy-start.1
  81.5 1.7 %copy.16 = f32[128,330]{0,1:T(8,128)} copy(f32[128,330]{1,0:T(8,128)} %get-tuple-element.16) | data formatting | bytes 337920
  83.2 0.0 copy-done.1
  83.2 0.0 copy-start.4
  83.2 0.0 copy-start
  83.2 0.6 copy.21
  83.8 0.0 copy-done.4
  83.9 0.5 copy.22
  84.4 0.0 copy-done
  84.4 0.0 copy-start.3
  84.4 0.6 copy.23
  85.0 0.0 copy-done.3
  85.1 0.5 copy.24
  (1 shorter events, 0.0 us)
Async XLA Ops:
  0.6 0.7 copy-start.2
  81.5 1.8 %copy-start.1 = (bf16[1,64,512]{2,1,0:T(8,128)(2,1)S(1)}, bf16[1,64,512]{2,1,0:T(8,128)(2,1)}, u32[]{:S(2)}) copy-start(bf16[1,64,512]{2,1,0:T(8,128)(2,1)} %get-tuple-element.25) | copy-start | bytes 196612
  83.2 0.7 copy-start.4
  83.2 1.2 %copy-start = (f32[64,330]{1,0:T(8,128)S(1)}, f32[64,330]{1,0:T(8,128)}, u32[]{:S(2)}) copy-start(f32[64,330]{1,0:T(8,128)} %get-tuple-element.28) | copy-start | bytes 253444
  84.4 0.7 copy-start.3

commit v3 on v2

--- a/solution.py
+++ b/solution.py
@@ -11,10 +11,15 @@
 MESH = pl.DeviceIdType.MESH
 HOPS = 8
 RS_EARLY, AG_EARLY, RS_LATE, AG_LATE, GROUPS = 8, 9, 10, 11, 12
+NY, NZ, NC = 4, 8, 2
 
 
 def mm(a, b):
     return jnp.dot(a, b, preferred_element_type=F32)
+
+
+def mm_t1(a, b):
+    return lax.dot_general(a, b, (((1,), (1,)), ((), ())), preferred_element_type=F32)
 
 
 def turn(a):
@@ -47,27 +52,52 @@
 
 def kernel(
     n_dom, n_snap, width, fin, chans, halo, factor,
+    *refs,
+):
+    sources, refs = refs[:10], refs[10:]
+    landed, refs = refs[-11:-1], refs[:-11] + refs[-1:]
+    copies = [
+        pltpu.make_async_copy(src, dst, refs[-1].at[at]) for at, (src, dst) in enumerate(zip(sources, landed))
+    ]
+    for copy in copies:
+        copy.start()
+    step(n_dom, n_snap, width, fin, chans, halo, factor, copies, *landed, *refs[:-1])
+
+
+def step(
+    n_dom, n_snap, width, fin, chans, halo, factor, copies,
     readings_ref, previous_ref, upstream_ref, gw_ref, gb_ref, cw_ref, cb_ref, nb_ref, ew_ref, sr_ref,
     state_ref, gate_out, gate_bias_out, cand_out, cand_bias_out,
     sp, ml, wl, sw, held, upward, scale_f, scale_a, local, wide, states, mixed, field, wg, wc, bg, bc,
     send_w, recv_w, send_n, recv_n, ssem, rsem, osem, rows,
-    early, late, piece_e, piece_l, snap_send, snap_recv, snap_s, snap_r, back_pick,
+    early, late, piece_e, piece_l, snap_send, snap_recv, snap_s, snap_r, back_pick, pick, bias2,
 ):
     me = lax.axis_index("dom")
     barrier = pltpu.get_barrier_semaphore()
 
-    def peer_of(k):
-        return (me + k) % n_dom
-
-    def greet(k, c):
-        pl.semaphore_signal(barrier, inc=1, device_id={"dom": peer_of(k)}, device_id_type=MESH)
-        return c
-
-    lax.fori_loop(1, n_dom, greet, 0)
+    my_core, my_z, my_y = me % NC, me // NC % NZ, me // (NC * NZ)
+
+    def each_peer(visit):
+        def ring(t, c):
+            z = (my_z + NZ + NZ // 2 + (t + 1) // 2 * (1 - t % 2 * 2)) % NZ
+            for dy in (2, 1, 3, 0):
+                for dc in range(NC):
+                    visit(((my_y + dy) % NY * NZ + z) * NC + (my_core + dc) % NC)
+            return c
+
+        lax.fori_loop(0, NZ - 1, ring, 0)
+        for dy in (2, 1, 3, 0):
+            for dc in range(NC):
+                if dy or dc:
+                    visit(((my_y + dy) % NY * NZ + my_z) * NC + (my_core + dc) % NC)
+
+    each_peer(lambda peer: pl.semaphore_signal(barrier, inc=1, device_id={"dom": peer}, device_id_type=MESH))
     mine = lax.axis_index("snap")
     for k in range(1, n_snap):
         pl.semaphore_signal(barrier, inc=1, device_id={"snap": (mine + k) % n_snap}, device_id_type=MESH)
 
+    for copy in copies:
+        copy.wait()
     lane128 = lanes(width, 128)
     low128 = lane128 < 64
 
@@ -115,27 +145,25 @@
     def send_all(group):
         src, dst = send_buf(group), recv_buf(group)
 
-        def go(k, c):
+        def go(peer):
             pltpu.make_async_remote_copy(
-                src.at[:, peer_of(k)], dst.at[:, me], ssem.at[group], rsem.at[group],
-                device_id={"dom": peer_of(k)}, device_id_type=MESH,
+                src.at[:, peer], dst.at[:, me], ssem.at[group], rsem.at[group],
+                device_id={"dom": peer}, device_id_type=MESH,
             ).start()
-            return c
-
-        lax.fori_loop(1, n_dom, go, 0)
+
+        each_peer(go)
         pltpu.make_async_copy(src.at[:, me], dst.at[:, me], osem.at[group]).start()
 
     def spread_piece(group, src):
         dst = recv_buf(group)
 
-        def go(k, c):
+        def go(peer):
             pltpu.make_async_remote_copy(
                 src, dst.at[:, me], ssem.at[group], rsem.at[group],
-                device_id={"dom": peer_of(k)}, device_id_type=MESH,
+                device_id={"dom": peer}, device_id_type=MESH,
             ).start()
-            return c
-
-        lax.fori_loop(1, n_dom, go, 0)
+
+        each_peer(go)
         pltpu.make_async_copy(src, dst.at[:, me], osem.at[group]).start()
 
     def launch(hop, values):
@@ -239,29 +267,28 @@
         deg_in = deg_in + wts[d]
     inv_in = 1.0 / deg_in
 
-    cols = gw_ref.shape[1]
-    pick = (
-        lax.broadcasted_iota(jnp.int32, (cols, 512), 0) == forward_map(lanes(1, 512), chans, fin)
-    )
-    pick = jnp.where(pick, 1.0, 0.0).astype(BF16)
-    pick_b = (
-        lax.broadcasted_iota(jnp.int32, (cols, 384), 0) == backward_map(lanes(1, 384), chans, fin)
-    )
-    pick_b = jnp.where(pick_b, 1.0, 0.0).astype(BF16)
+    cols = gw_ref.shape[0]
+    pick[...] = jnp.where(
+        lax.broadcasted_iota(jnp.int32, (cols, 512), 0) == forward_map(lanes(1, 512), chans, fin), 1.0, 0.0
+    ).astype(BF16)
     column = lax.broadcasted_iota(jnp.int32, (512, 1), 0)
-    back_pick[...] = jnp.where(
-        lanes(512, 384) == forward_map(column, chans, fin), 1.0, 0.0
+    back_pick[...] = jnp.where(lanes(512, cols) == forward_map(column, chans, fin), 1.0, 0.0).astype(BF16)
+    adjoint_pick = jnp.where(
+        lanes(384, cols) == backward_map(column[:384], chans, fin), 1.0, 0.0
     ).astype(BF16)
     gate_w = gw_ref[...]
     cand_w = cw_ref[...]
-    gate_f = mm(gate_w, pick)
-    cand_f = mm(cand_w, pick)
-    r, u = gate_f[:64], gate_f[64:]
-    wg[...] = jnp.transpose(jnp.concatenate([r, r, u, u], axis=0)).astype(BF16)
-    wc[...] = jnp.transpose(jnp.concatenate([cand_f, cand_f], axis=0)).astype(BF16)
-    bg[...] = mm(gate_w, pick_b).astype(BF16)
-    bc[:64, :] = mm(cand_w, pick_b).astype(BF16)
+    gate_f = mm(back_pick[...], gate_w)
+    turned = pltpu.roll(gate_f, 64, 1)
+    low512 = lanes(512, 128) < 64
+    wg[:, :128] = jnp.where(low512, gate_f, turned).astype(BF16)
+    wg[:, 128:] = jnp.where(low512, turned, gate_f).astype(BF16)
+    wc[...] = mm_t1(back_pick[...], jnp.concatenate([cand_w, cand_w], axis=0)).astype(BF16)
+    bg[...] = jnp.transpose(mm(adjoint_pick, gate_w)).astype(BF16)
+    bc[:64, :] = mm_t1(cand_w, adjoint_pick).astype(BF16)
     bc[64:, :] = jnp.zeros((64, 384), BF16)
+    bias2[0:1, :64] = cb_ref[...]
+    bias2[0:1, 64:] = cb_ref[...]
 
     wide[...] = near(start.astype(BF16))
     await_recv(0)
@@ -307,7 +334,7 @@
     await_recv(3)
     raw = far(3) + local[...]
     mixed[:, 128:256] = (2.0 * raw * scale_f[...] - scaled.astype(F32)).astype(BF16)
-    cand = jnp.tanh(mm(mixed[...], wc[...]) + cb_ref[...])
+    cand = jnp.tanh(mm(mixed[...], wc[...]) + bias2[0:1, :])
     cand_grad = (upward[...] * (1.0 - update) * (1.0 - cand * cand)).astype(BF16)
 
     update_part = upward[...] * (held[...] - cand) * update * (1.0 - update)
@@ -365,26 +392,28 @@
     await_recv(AG_EARLY)
     bias_row = jnp.where(lanes(8, 128) == 64 + fin, 1.0, 0.0).astype(BF16)
 
-    def put(tiles, weight_out, bias_out):
-        total = mm(tiles[0], back_pick[:128, :])
-        for tile in range(1, 4):
-            total = total + mm(tiles[tile], back_pick[tile * 128 : tile * 128 + 128, :])
-        weight_out[...] = total[:, : weight_out.shape[1]] * factor
-        bias = lax.dot_general(bias_row, tiles[2], (((1,), (1,)), ((), ())), preferred_element_type=F32)
-        bias_out[...] = bias[0:1, :] * factor
-
-    put([gathered(AG_EARLY, tile, 128)[:64] for tile in range(4)], cand_out, cand_bias_out)
+    def put_bias(tiles, bias_out):
+        bias_out[...] = mm_t1(bias_row, tiles[2])[0:1, :] * factor
+
+    tiles = [gathered(AG_EARLY, tile, 128)[:64] for tile in range(4)]
+    total = mm(tiles[0], back_pick[:128, :])
+    for tile in range(1, 4):
+        total = total + mm(tiles[tile], back_pick[tile * 128 : tile * 128 + 128, :])
+    cand_out[...] = total * factor
+    put_bias(tiles, cand_bias_out)
     state_part = last_hop(7)
     result = upward[...] * update + scaled_grad * reset + state_part
     state_ref[0] = jnp.transpose(result)[:64, :].astype(BF16)
     await_recv(AG_LATE)
-    put(
-        [
-            jnp.concatenate([gathered(AG_LATE, tile, 64), gathered(AG_EARLY, tile, 128)[64:]], axis=0)
-            for tile in range(4)
-        ],
-        gate_out, gate_bias_out,
-    )
+    tiles = [
+        jnp.concatenate([gathered(AG_LATE, tile, 64), gathered(AG_EARLY, tile, 128)[64:]], axis=0)
+        for tile in range(4)
+    ]
+    total = mm_t1(pick[:, :128], tiles[0])
+    for tile in range(1, 4):
+        total = total + mm_t1(pick[:, tile * 128 : tile * 128 + 128], tiles[tile])
+    gate_out[...] = total * factor
+    put_bias(tiles, gate_bias_out)
 
     for group in range(GROUPS):
         rest = recv_buf(group).at[:, pl.ds(0, n_dom - 1)]
@@ -409,16 +438,17 @@
             kernel(n_dom, n_snap, width, fin, chans, halo, factor, *refs)
 
         cols = gw.shape[1]
+        arrays = (readings, previous, upstream, gw.T, gb.reshape(1, -1), cw, cb.reshape(1, -1), nb, ew, sr)
         state, gate, gate_b, cand, cand_b = pl.pallas_call(
             run,
             out_shape=(
                 jax.ShapeDtypeStruct((1, hidden, width), BF16),
-                jax.ShapeDtypeStruct((2 * hidden, cols), F32),
+                jax.ShapeDtypeStruct((cols, 2 * hidden), F32),
                 jax.ShapeDtypeStruct((1, 2 * hidden), F32),
                 jax.ShapeDtypeStruct((hidden, cols), F32),
                 jax.ShapeDtypeStruct((1, hidden), F32),
             ),
-            in_specs=[vmem] * 10,
+            in_specs=[pl.BlockSpec(memory_space=pl.ANY)] * 10,
             out_specs=(vmem,) * 5,
             scratch_shapes=[
                 pltpu.VMEM((2 * halo, width), BF16),
@@ -454,11 +484,15 @@
                 pltpu.VMEM((2, n_snap, 8, 128), F32),
                 pltpu.SemaphoreType.DMA((2,)),
                 pltpu.SemaphoreType.DMA((2,)),
-                pltpu.VMEM((512, 384), BF16),
+                pltpu.VMEM((512, cols), BF16),
+                pltpu.VMEM((cols, 512), BF16),
+                pltpu.VMEM((8, 128), F32),
+                *(pltpu.VMEM(array.shape, array.dtype) for array in arrays),
+                pltpu.SemaphoreType.DMA((len(arrays),)),
             ],
             compiler_params=pltpu.CompilerParams(collective_id=0, has_side_effects=True),
-        )(readings, previous, upstream, gw, gb.reshape(1, -1), cw, jnp.tile(cb.reshape(1, -1), (1, 2)), nb, ew, sr)
-        return state, gate, gate_b.reshape(-1), cand, cand_b.reshape(-1)
+        )(*arrays)
+        return state, gate.T, gate_b.reshape(-1), cand, cand_b.reshape(-1)
 
     in_specs = (
         P("snap", None, "dom"), P("snap", None, "dom"), P("snap", None, "dom"),

time: 85.8 us -> 78.1 us (0.910)
  Pallas kernels: 77.9 us -> 72.4 us
  local copies, waits for them, and re-layouts: 6.99 us -> 4.82 us
    pallas_call x1, Pallas kernels: 77.9 us -> 72.4 us  [body(): pl.pallas_call(run, out_shape=(jax.ShapeDtypeStruct((1, hidden, width), B...]
    unnamed x16 -> x11, local copies, waits for them, and re-layouts: 6.4 us -> 4.82 us
where the time goes in v3:
time: 78.1 us; the launch traced here: 77.9 us
  Pallas kernels  72.4 us (93%)
  local copies, waits for them, and re-layouts  4.82 us (6%)
    pallas_call x1, Pallas kernels, body(): pl.pallas_call(run, out_shape=(jax.ShapeDtypeStruct((1, hidden, width), B...  72.4 us
    unnamed x11, local copies, waits for them, and re-layouts  4.82 us

profile of v3, /device:TPU:1, one launch (start us, length us, event | category | flops | bytes accessed | tf_op | source)
XLA Modules:
  0.0 77.9 jit_solution(7215219903063387313)
XLA Ops:
  0.6 72.4 %shard_map.137 = (bf16[1,64,512]{2,1,0:T(8,128)(2,1)}, f32[330,128]{1,0:T(8,128)}, f32[1,128]{1,0:T(1,128)}, f32[64,330]{1,0:T(8,128)}, f32[1,64]{1,0:T(1,128)}) custom-call(bf16[1,2,512]{2,1,0:T(2,128)(2,1)} %refs_0_.1, bf16[1,64,512]{2,1,0:T(8,128)(2,1)} %refs_1_.1, bf16[1,64,512]{2,1,0:T(8,128)(2,1)} %refs_2_.1, bf16[330,128]{1,0:T(8,128)(2,1)} %bitcast.7, ...), custom_call_target="tpu_custom_call" | custom-call | tf_op jit(solution)/shard_map/pallas_call | solution.py:442
  73.1 1.5 %copy.20 = bf16[1,64,512]{2,1,0:T(8,128)(2,1)} copy(bf16[1,64,512]{2,1,0:T(8,128)(2,1)} %get-tuple-element.20) | data formatting | bytes 131072
  74.5 0.0 copy-start.2
  74.5 0.0 copy-start
  74.5 1.6 %copy.21 = f32[128,330]{0,1:T(8,128)} copy(f32[128,330]{0,1:T(8,128)} %bitcast.6) | data formatting | bytes 337920
  76.2 0.0 copy-done.2
  76.2 0.5 copy.22
  76.7 0.0 copy-done
  76.7 0.0 copy-start.1
  76.7 0.6 copy.23
  77.3 0.0 copy-done.1
  77.4 0.5 copy.24
Async XLA Ops:
  74.5 1.6 %copy-start.2 = (f32[1,128]{1,0:T(1,128)S(1)}, f32[1,128]{1,0:T(1,128)}, u32[]{:S(2)}) copy-start(f32[1,128]{1,0:T(1,128)} %get-tuple-element.12) | copy-start | bytes 1540
  74.5 2.2 %copy-start = (f32[64,330]{1,0:T(8,128)S(1)}, f32[64,330]{1,0:T(8,128)}, u32[]{:S(2)}) copy-start(f32[64,330]{1,0:T(8,128)} %get-tuple-element.23) | copy-start | bytes 253444
  76.7 0.7 copy-start.1

commit v4 on v3

--- a/solution.py
+++ b/solution.py
@@ -68,9 +68,10 @@
     n_dom, n_snap, width, fin, chans, halo, factor, copies,
     readings_ref, previous_ref, upstream_ref, gw_ref, gb_ref, cw_ref, cb_ref, nb_ref, ew_ref, sr_ref,
     state_ref, gate_out, gate_bias_out, cand_out, cand_bias_out,
-    sp, ml, wl, sw, held, upward, scale_f, scale_a, local, wide, states, mixed, field, wg, wc, bg, bc,
+    sp, near_m, far_m, held, upward, scale_f, scale_a, local, wide, states, mixed, field, wg, wc, bg, bc,
     send_w, recv_w, send_n, recv_n, ssem, rsem, osem, rows,
     early, late, piece_e, piece_l, snap_send, snap_recv, snap_s, snap_r, back_pick, pick, bias2,
+    gate_r, gate_u, slope_c, slope_r, part, inner_v,
 ):
     me = lax.axis_index("dom")
     barrier = pltpu.get_barrier_semaphore()
@@ -117,7 +118,7 @@
     columns = jnp.transpose(rows[1])
 
     rows_sel = columns[:halo, 16:17].astype(jnp.int32)
-    sp[:halo, :] = jnp.where(lanes(halo, width) == rows_sel, 1.0, 0.0).astype(BF16)
+    sp[:, width:] = jnp.where(lanes(halo, width) == rows_sel, 1.0, 0.0).astype(BF16)
 
     def push_block(first, rows):
         here = lax.broadcasted_iota(jnp.int32, (rows, width), 0) + first
@@ -127,7 +128,7 @@
         return total
 
     edge_sums = push_block(width, halo)
-    sp[halo:, :] = edge_sums.astype(BF16)
+    sp[:, :width] = edge_sums.astype(BF16)
     deg_halo = jnp.sum(edge_sums, axis=1, keepdims=True)
     deg_high = deg_halo.astype(BF16).astype(F32)
     deg_rest = deg_halo - deg_high
@@ -166,12 +167,13 @@
         each_peer(go)
         pltpu.make_async_copy(src, dst.at[:, me], osem.at[group]).start()
 
+    def halves(values):
+        low = jnp.where(lanes(*values.shape) % 128 < 64, 1.0, 0.0).astype(BF16)
+        return jnp.concatenate([values * low, values * (1.0 - low)], axis=0)
+
     def launch(hop, values):
         span = values.shape[1]
-        mixed_rows = mm(sp[...], values)
-        out = jnp.where(
-            lanes(halo, span) % 128 < 64, mixed_rows[halo:, :], mixed_rows[:halo, :]
-        )
+        out = mm(sp[...], halves(values))
         if hop == 0:
             lane = lanes(halo, span)
             out = jnp.where(lane == 128 + fin, deg_high, jnp.where(lane == 128 + fin + 1, deg_rest, out))
@@ -185,9 +187,7 @@
         send_all(hop)
 
     def near(values):
-        span = values.shape[1]
-        low = lanes(width, span) % 128 < 64
-        return jnp.where(low, mm(ml[...], values), mm(wl[...], values))
+        return mm(near_m[...], halves(values))
 
     def await_recv(hop):
         dst = recv_buf(hop)
@@ -233,12 +233,9 @@
 
     def far(hop):
         dst = recv_buf(hop)
-        span = 256 if hop < 2 else 128
-        got = [dst.at[part].reshape(halo, 128)[...] for part in range(span // 128)]
+        got = [dst.at[part].reshape(halo, 128)[...] for part in range(dst.shape[0])]
         got = got[0] if len(got) == 1 else jnp.concatenate(got, axis=1)
-        both = mm(sw[...], got)
-        low = lanes(width, span) % 128 < 64
-        return jnp.where(low, both[:width, :], both[width:, :])
+        return mm(far_m[...], halves(got))
 
     start = jnp.concatenate([held[...], extra], axis=1)
     launch(0, start.astype(BF16))
@@ -251,15 +248,15 @@
         for d in range(degs):
             total = total + jnp.where(srcs[d][first : first + 128] == here, wts[d][first : first + 128], 0.0)
         total = total.astype(BF16)
-        wl[first : first + 128, :] = total[:, :width]
-        sw[width + first : width + first + 128, :] = total[:, width:]
+        near_m[first : first + 128, width:] = total[:, :width]
+        far_m[first : first + 128, halo:] = total[:, width:]
     deg_near = []
     for first in range(0, width, 128):
         block = push_block(first, 128)
-        ml[first : first + 128, :] = block.astype(BF16)
+        near_m[first : first + 128, :width] = block.astype(BF16)
         deg_near.append(jnp.sum(block, axis=1, keepdims=True))
     deg_near = jnp.concatenate(deg_near, axis=0)
-    sw[:width, :] = jnp.where(
+    far_m[:, :halo] = jnp.where(
         lax.broadcasted_iota(jnp.int32, (width, halo), 0) == sr_ref[...], 1.0, 0.0
     ).astype(BF16)
     deg_in = wts[0]
@@ -308,6 +305,13 @@
     )
     states[:, 256:384] = ones.astype(BF16)
     wide[...] = near(second_in)
+    bias = jnp.broadcast_to(gb_ref[...], (width, 128))
+    turned = pltpu.roll(bias, 64, 1)
+    local[...] = (
+        mm(states[:, :128], wg[:128, :128])
+        + mm(states[:, 256:384], wg[256:384, :128])
+        + jnp.where(low128, bias, turned)
+    )
     await_recv(1)
     raw = far(1) + wide[...]
     states[:, 128:256] = (2.0 * raw[:, :128] * scale_f[...] - held[...]).astype(BF16)
@@ -315,29 +319,32 @@
     tail = first_extra.astype(BF16).astype(F32) + pltpu.roll(second_extra.astype(BF16).astype(F32), fin, 1)
     states[:, 384:] = tail.astype(BF16)
 
-    gates = mm(states[...], wg[...])
-    bias = jnp.broadcast_to(gb_ref[...], (width, 128))
-    turned = pltpu.roll(bias, 64, 1)
-    reset = jax.nn.sigmoid(gates[:, :128] + jnp.where(low128, bias, turned))
-    update = jax.nn.sigmoid(gates[:, 128:] + jnp.where(low128, turned, bias))
+    reset = jax.nn.sigmoid(
+        local[...] + mm(states[:, 128:256], wg[128:256, :128]) + mm(states[:, 384:], wg[384:, :128])
+    )
     scaled = (reset * held[...]).astype(BF16)
-
     launch(2, scaled)
+    local[...] = near(scaled)
+    update = jax.nn.sigmoid(mm(states[...], wg[:, 128:]) + jnp.where(low128, turned, bias))
+    gate_r[...] = reset
+    gate_u[...] = update
+    slope_c[...] = upward[...] * (1.0 - update)
+    slope_r[...] = held[...] * reset * (1.0 - reset)
     mixed[:, 256:384] = jnp.where(low128, scaled, states[:, 256:384])
     mixed[:, 384:] = states[:, 384:]
-    local[...] = near(scaled)
     await_recv(2)
     hop_one = ((far(2) + local[...]) * scale_f[...]).astype(BF16)
     launch(3, hop_one)
     mixed[:, :128] = hop_one
     local[...] = near(hop_one)
+    part[...] = (
+        mm(mixed[:, :128], wc[:128, :]) + mm(mixed[:, 256:], wc[256:, :]) + bias2[0:1, :]
+    )
     await_recv(3)
     raw = far(3) + local[...]
     mixed[:, 128:256] = (2.0 * raw * scale_f[...] - scaled.astype(F32)).astype(BF16)
-    cand = jnp.tanh(mm(mixed[...], wc[...]) + bias2[0:1, :])
-    cand_grad = (upward[...] * (1.0 - update) * (1.0 - cand * cand)).astype(BF16)
-
-    update_part = upward[...] * (held[...] - cand) * update * (1.0 - update)
+    cand = jnp.tanh(part[...] + mm(mixed[:, 128:256], wc[128:256, :]))
+    cand_grad = (slope_c[...] * (1.0 - cand * cand)).astype(BF16)
 
     def outer_hop(grad, weights, hop):
         outer = mm(grad, weights[:, :128])
@@ -347,12 +354,12 @@
 
     def inner_hop(grad, weights, hop, outer, values, meanwhile):
         local[...] = near(values)
-        inner = mm(grad, weights[:, 128:256])
+        inner_v[...] = mm(grad, weights[:, 128:256])
         field[...] = mm(grad, weights[:, 256:384]) - outer - pltpu.roll(outer, 64, 1)
         meanwhile()
         await_recv(hop)
         raw = far(hop) + local[...]
-        values = ((inner + 2.0 * raw) * scale_a[...]).astype(BF16)
+        values = ((inner_v[...] + 2.0 * raw) * scale_a[...]).astype(BF16)
         launch(hop + 1, values)
         local[...] = near(values)
 
@@ -362,6 +369,8 @@
         return field[...] + raw + pltpu.roll(raw, 64, 1)
 
     def early_sums():
+        update_part = upward[...] * (held[...] - cand) * gate_u[...] * (1.0 - gate_u[...])
+        part[...] = update_part
         grads = turn(jnp.where(low128, cand_grad.astype(F32), update_part)).astype(BF16)
         by_cand = mm(grads[:64, :], mixed[...])
         by_update = mm(grads[64:, :], states[...])
@@ -375,18 +384,19 @@
     outer, values = outer_hop(cand_grad, bc, 4)
     inner_hop(cand_grad, bc, 4, outer, values, early_sums)
     reduce_pieces(RS_EARLY, 0)
+    finish_pieces(AG_EARLY, 0, piece_e)
     scaled_grad = last_hop(5)
-    reset_part = scaled_grad * held[...] * reset * (1.0 - reset)
-    gate_grad = jnp.where(low128, reset_part, update_part).astype(BF16)
-    outer, values = outer_hop(gate_grad, bg, 6)
+    gate_grad = jnp.where(low128, scaled_grad * slope_r[...], part[...]).astype(BF16)
     by_reset = mm(turn(gate_grad)[:64, :].astype(BF16), states[...])
     for tile in range(4):
         late.at[0, 0].reshape(halo, 128)[tile * 64 : tile * 64 + 64, :] = by_reset[
             :, tile * 128 : tile * 128 + 128
         ].astype(BF16)
     send_all(RS_LATE)
-    inner_hop(gate_grad, bg, 6, outer, values, lambda: finish_pieces(AG_EARLY, 0, piece_e))
-    reduce_pieces(RS_LATE, 1)
+    outer, values = outer_hop(gate_grad, bg, 6)
+    part[...] = upward[...] * gate_u[...] + scaled_grad * gate_r[...]
+    inner_hop(gate_grad, bg, 6, outer, values, lambda: reduce_pieces(RS_LATE, 1))
+    field[...] = field[...] + part[...]
     finish_pieces(AG_LATE, 1, piece_l)
 
     await_recv(AG_EARLY)
@@ -401,9 +411,7 @@
         total = total + mm(tiles[tile], back_pick[tile * 128 : tile * 128 + 128, :])
     cand_out[...] = total * factor
     put_bias(tiles, cand_bias_out)
-    state_part = last_hop(7)
-    result = upward[...] * update + scaled_grad * reset + state_part
-    state_ref[0] = jnp.transpose(result)[:64, :].astype(BF16)
+    state_ref[0] = jnp.transpose(last_hop(7))[:64, :].astype(BF16)
     await_recv(AG_LATE)
     tiles = [
         jnp.concatenate([gathered(AG_LATE, tile, 64), gathered(AG_EARLY, tile, 128)[64:]], axis=0)
@@ -451,10 +459,9 @@
             in_specs=[pl.BlockSpec(memory_space=pl.ANY)] * 10,
             out_specs=(vmem,) * 5,
             scratch_shapes=[
-                pltpu.VMEM((2 * halo, width), BF16),
-                pltpu.VMEM((width, width), BF16),
-                pltpu.VMEM((width, width), BF16),
-                pltpu.VMEM((2 * width, halo), BF16),
+                pltpu.VMEM((halo, 2 * width), BF16),
+                pltpu.VMEM((width, 2 * width), BF16),
+                pltpu.VMEM((width, 2 * halo), BF16),
                 pltpu.VMEM((width, 128), F32),
                 pltpu.VMEM((width, 128), F32),
                 pltpu.VMEM((width, 128), F32),
@@ -487,11 +494,24 @@
                 pltpu.VMEM((512, cols), BF16),
                 pltpu.VMEM((cols, 512), BF16),
                 pltpu.VMEM((8, 128), F32),
+                *[pltpu.VMEM((width, 128), F32)] * 6,
                 *(pltpu.VMEM(array.shape, array.dtype) for array in arrays),
                 pltpu.SemaphoreType.DMA((len(arrays),)),
             ],
             compiler_params=pltpu.CompilerParams(collective_id=0, has_side_effects=True),
         )(*arrays)
+        results = (state, gate, gate_b, cand, cand_b)
+
+        def write(*refs):
+            for src, dst in zip(refs[: len(results)], refs[len(results) :]):
+                dst[...] = src[...]
+
+        state, gate, gate_b, cand, cand_b = pl.pallas_call(
+            write,
+            out_shape=tuple(jax.ShapeDtypeStruct(array.shape, array.dtype) for array in results),
+            in_specs=[vmem] * len(results),
+            out_specs=(vmem,) * len(results),
+        )(*results)
         return state, gate.T, gate_b.reshape(-1), cand, cand_b.reshape(-1)
 
     in_specs = (

time: 78.1 us -> 73.2 us (0.937)
  local copies, waits for them, and re-layouts: 4.82 us -> 0 us
    unnamed x11 -> x0, local copies, waits for them, and re-layouts: 4.82 us -> none
    pallas_call x0 -> x1, Pallas kernels: none -> 1.72 us  [body(): pl.pallas_call(write, out_shape=tuple((jax.ShapeDtypeStruct(array.shape,...]
    pallas_call x1, Pallas kernels: 72.4 us -> 70.7 us  [body(): pl.pallas_call(run, out_shape=(jax.ShapeDtypeStruct((1, hidden, width), B...]
where the time goes in v4:
time: 73.2 us; the launch traced here: 73.1 us
  Pallas kernels  72.4 us (99%)
    pallas_call x1, Pallas kernels, body(): pl.pallas_call(run, out_shape=(jax.ShapeDtypeStruct((1, hidden, width), B...  70.7 us
    pallas_call x1, Pallas kernels, body(): pl.pallas_call(write, out_shape=tuple((jax.ShapeDtypeStruct(array.shape,...  1.72 us

profile of v4, /device:TPU:1, one launch (start us, length us, event | category | flops | bytes accessed | tf_op | source)
XLA Modules:
  0.0 73.1 jit_solution(11234623416921113714)
XLA Ops:
  0.6 70.7 %shard_map.137 = (bf16[1,64,512]{2,1,0:T(8,128)(2,1)}, f32[330,128]{1,0:T(8,128)}, f32[1,128]{1,0:T(1,128)}, f32[64,330]{1,0:T(8,128)}, f32[1,64]{1,0:T(1,128)}) custom-call(bf16[1,2,512]{2,1,0:T(2,128)(2,1)} %refs_0_.1, bf16[1,64,512]{2,1,0:T(8,128)(2,1)} %refs_1_.1, bf16[1,64,512]{2,1,0:T(8,128)(2,1)} %refs_2_.1, bf16[330,128]{1,0:T(8,128)(2,1)} %bitcast.6, ...), custom_call_target="tpu_custom_call" | custom-call | tf_op jit(solution)/shard_map/pallas_call | solution.py:450
  71.4 1.7 %shard_map.138 = (bf16[1,64,512]{2,1,0:T(8,128)(2,1)}, f32[330,128]{1,0:T(8,128)}, f32[1,128]{1,0:T(1,128)}, f32[64,330]{1,0:T(8,128)}, f32[1,64]{1,0:T(1,128)}) custom-call(bf16[1,64,512]{2,1,0:T(8,128)(2,1)} %get-tuple-element.15.refs_0_, f32[330,128]{1,0:T(8,128)} %get-tuple-element.16.refs_1_, f32[1,128]{1,0:T(1,128)} %get-tuple-element.17.refs_2_, ...), custom_call_target="tpu_custom_call" | custom-call | tf_op jit(solution)/shard_map/pallas_call | solution.py:509

commit v5 on v4

--- a/solution.py
+++ b/solution.py
@@ -68,10 +68,10 @@
     n_dom, n_snap, width, fin, chans, halo, factor, copies,
     readings_ref, previous_ref, upstream_ref, gw_ref, gb_ref, cw_ref, cb_ref, nb_ref, ew_ref, sr_ref,
     state_ref, gate_out, gate_bias_out, cand_out, cand_bias_out,
-    sp, near_m, far_m, held, upward, scale_f, scale_a, local, wide, states, mixed, field, wg, wc, bg, bc,
+    sp, ml, wl, sw, comp_f, comp_a, held, upward, scale_f, scale_a, local, wide, states, mixed, field, wg, wc, bg, bc,
     send_w, recv_w, send_n, recv_n, ssem, rsem, osem, rows,
     early, late, piece_e, piece_l, snap_send, snap_recv, snap_s, snap_r, back_pick, pick, bias2,
-    gate_r, gate_u, slope_c, slope_r, part, inner_v,
+    gate_r, gate_u, slope_c, slope_r, part, inner_v, ahead,
 ):
     me = lax.axis_index("dom")
     barrier = pltpu.get_barrier_semaphore()
@@ -118,7 +118,7 @@
     columns = jnp.transpose(rows[1])
 
     rows_sel = columns[:halo, 16:17].astype(jnp.int32)
-    sp[:, width:] = jnp.where(lanes(halo, width) == rows_sel, 1.0, 0.0).astype(BF16)
+    sp[:halo, :] = jnp.where(lanes(halo, width) == rows_sel, 1.0, 0.0).astype(BF16)
 
     def push_block(first, rows):
         here = lax.broadcasted_iota(jnp.int32, (rows, width), 0) + first
@@ -128,7 +128,7 @@
         return total
 
     edge_sums = push_block(width, halo)
-    sp[:, :width] = edge_sums.astype(BF16)
+    sp[halo:, :] = edge_sums.astype(BF16)
     deg_halo = jnp.sum(edge_sums, axis=1, keepdims=True)
     deg_high = deg_halo.astype(BF16).astype(F32)
     deg_rest = deg_halo - deg_high
@@ -167,13 +167,12 @@
         each_peer(go)
         pltpu.make_async_copy(src, dst.at[:, me], osem.at[group]).start()
 
-    def halves(values):
-        low = jnp.where(lanes(*values.shape) % 128 < 64, 1.0, 0.0).astype(BF16)
-        return jnp.concatenate([values * low, values * (1.0 - low)], axis=0)
-
-    def launch(hop, values):
-        span = values.shape[1]
-        out = mm(sp[...], halves(values))
+    def to_send(values):
+        rows = mm(sp[...], values)
+        return jnp.where(lanes(halo, values.shape[1]) % 128 < 64, rows[halo:, :], rows[:halo, :])
+
+    def launch(hop, out):
+        span = out.shape[1]
         if hop == 0:
             lane = lanes(halo, span)
             out = jnp.where(lane == 128 + fin, deg_high, jnp.where(lane == 128 + fin + 1, deg_rest, out))
@@ -187,7 +186,8 @@
         send_all(hop)
 
     def near(values):
-        return mm(near_m[...], halves(values))
+        low = lanes(*values.shape) % 128 < 64
+        return jnp.where(low, mm(ml[...], values), mm(wl[...], values))
 
     def await_recv(hop):
         dst = recv_buf(hop)
@@ -231,14 +231,22 @@
         at = tile * count
         return recv_buf(group).at[at // halo].reshape(halo, 128)[at % halo : at % halo + count, :]
 
-    def far(hop):
+    def arrived(hop):
         dst = recv_buf(hop)
         got = [dst.at[part].reshape(halo, 128)[...] for part in range(dst.shape[0])]
-        got = got[0] if len(got) == 1 else jnp.concatenate(got, axis=1)
-        return mm(far_m[...], halves(got))
+        return got[0] if len(got) == 1 else jnp.concatenate(got, axis=1)
+
+    def far(got):
+        both = mm(sw[...], got)
+        low = lanes(width, got.shape[1]) % 128 < 64
+        return jnp.where(low, both[:width, :], both[width:, :])
+
+    def onward(got, composed):
+        rows = mm(composed[...], got)
+        return jnp.where(lanes(halo, 128) < 64, rows[halo:, :], rows[:halo, :])
 
     start = jnp.concatenate([held[...], extra], axis=1)
-    launch(0, start.astype(BF16))
+    launch(0, to_send(start.astype(BF16)))
 
     wts = [columns[:, 8 + d : 9 + d] for d in range(degs)]
     srcs = [columns[:, d : d + 1].astype(jnp.int32) for d in range(degs)]
@@ -248,15 +256,15 @@
         for d in range(degs):
             total = total + jnp.where(srcs[d][first : first + 128] == here, wts[d][first : first + 128], 0.0)
         total = total.astype(BF16)
-        near_m[first : first + 128, width:] = total[:, :width]
-        far_m[first : first + 128, halo:] = total[:, width:]
+        wl[first : first + 128, :] = total[:, :width]
+        sw[width + first : width + first + 128, :] = total[:, width:]
     deg_near = []
     for first in range(0, width, 128):
         block = push_block(first, 128)
-        near_m[first : first + 128, :width] = block.astype(BF16)
+        ml[first : first + 128, :] = block.astype(BF16)
         deg_near.append(jnp.sum(block, axis=1, keepdims=True))
     deg_near = jnp.concatenate(deg_near, axis=0)
-    far_m[:, :halo] = jnp.where(
+    sw[:width, :] = jnp.where(
         lax.broadcasted_iota(jnp.int32, (width, halo), 0) == sr_ref[...], 1.0, 0.0
     ).astype(BF16)
     deg_in = wts[0]
@@ -289,7 +297,7 @@
 
     wide[...] = near(start.astype(BF16))
     await_recv(0)
-    raw = far(0)
+    raw = far(arrived(0))
     deg_out = deg_near + raw[:, 128 + fin : 129 + fin] + raw[:, 129 + fin : 130 + fin]
     raw = raw + wide[...]
     inv_out = 1.0 / deg_out
@@ -299,7 +307,12 @@
     states[:, :128] = first_main
     first_extra = jnp.where(lane128 % 64 < fin, raw[:, 128:] * scale_f[...], 0.0)
     second_in = jnp.concatenate([first_main, first_extra.astype(BF16)], axis=1)
-    launch(1, second_in)
+    launch(1, to_send(second_in))
+    for comp, times, by_push, by_pull in ((comp_f, 1.0, inv_out, inv_in), (comp_a, 2.0, inv_in, inv_out)):
+        pushed = (sw[:width, :].astype(F32) * by_push).astype(BF16)
+        pulled = (sw[width:, :].astype(F32) * by_pull).astype(BF16)
+        comp[halo:, :] = (mm(sp[halo:, :], pushed) * times).astype(BF16)
+        comp[:halo, :] = (mm(sp[:halo, :], pulled) * times).astype(BF16)
     ones = jnp.where(
         low128, held[...], jnp.where(lane128 < 64 + fin, extra, jnp.where(lane128 == 64 + fin, 1.0, 0.0))
     )
@@ -313,7 +326,7 @@
         + jnp.where(low128, bias, turned)
     )
     await_recv(1)
-    raw = far(1) + wide[...]
+    raw = far(arrived(1)) + wide[...]
     states[:, 128:256] = (2.0 * raw[:, :128] * scale_f[...] - held[...]).astype(BF16)
     second_extra = 2.0 * raw[:, 128:] * scale_f[...] - extra
     tail = first_extra.astype(BF16).astype(F32) + pltpu.roll(second_extra.astype(BF16).astype(F32), fin, 1)
@@ -323,8 +336,10 @@
         local[...] + mm(states[:, 128:256], wg[128:256, :128]) + mm(states[:, 384:], wg[384:, :128])
     )
     scaled = (reset * held[...]).astype(BF16)
-    launch(2, scaled)
-    local[...] = near(scaled)
+    launch(2, to_send(scaled))
+    beside = near(scaled)
+    local[...] = beside
+    ahead[...] = to_send((beside * scale_f[...]).astype(BF16))
     update = jax.nn.sigmoid(mm(states[...], wg[:, 128:]) + jnp.where(low128, turned, bias))
     gate_r[...] = reset
     gate_u[...] = update
@@ -333,15 +348,16 @@
     mixed[:, 256:384] = jnp.where(low128, scaled, states[:, 256:384])
     mixed[:, 384:] = states[:, 384:]
     await_recv(2)
-    hop_one = ((far(2) + local[...]) * scale_f[...]).astype(BF16)
-    launch(3, hop_one)
+    got = arrived(2)
+    launch(3, ahead[...] + onward(got, comp_f))
+    hop_one = ((far(got) + local[...]) * scale_f[...]).astype(BF16)
     mixed[:, :128] = hop_one
     local[...] = near(hop_one)
     part[...] = (
         mm(mixed[:, :128], wc[:128, :]) + mm(mixed[:, 256:], wc[256:, :]) + bias2[0:1, :]
     )
     await_recv(3)
-    raw = far(3) + local[...]
+    raw = far(arrived(3)) + local[...]
     mixed[:, 128:256] = (2.0 * raw * scale_f[...] - scaled.astype(F32)).astype(BF16)
     cand = jnp.tanh(part[...] + mm(mixed[:, 128:256], wc[128:256, :]))
     cand_grad = (slope_c[...] * (1.0 - cand * cand)).astype(BF16)
@@ -349,23 +365,27 @@
     def outer_hop(grad, weights, hop):
         outer = mm(grad, weights[:, :128])
         values = (outer * scale_a[...]).astype(BF16)
-        launch(hop, values)
+        launch(hop, to_send(values))
         return outer, values
 
     def inner_hop(grad, weights, hop, outer, values, meanwhile):
-        local[...] = near(values)
-        inner_v[...] = mm(grad, weights[:, 128:256])
+        beside = near(values)
+        local[...] = beside
+        inner = mm(grad, weights[:, 128:256])
+        inner_v[...] = inner
+        ahead[...] = to_send(((inner + 2.0 * beside) * scale_a[...]).astype(BF16))
         field[...] = mm(grad, weights[:, 256:384]) - outer - pltpu.roll(outer, 64, 1)
         meanwhile()
         await_recv(hop)
-        raw = far(hop) + local[...]
+        got = arrived(hop)
+        launch(hop + 1, ahead[...] + onward(got, comp_a))
+        raw = far(got) + local[...]
         values = ((inner_v[...] + 2.0 * raw) * scale_a[...]).astype(BF16)
-        launch(hop + 1, values)
         local[...] = near(values)
 
     def last_hop(hop):
         await_recv(hop)
-        raw = far(hop) + local[...]
+        raw = far(arrived(hop)) + local[...]
         return field[...] + raw + pltpu.roll(raw, 64, 1)
 
     def early_sums():
@@ -384,7 +404,6 @@
     outer, values = outer_hop(cand_grad, bc, 4)
     inner_hop(cand_grad, bc, 4, outer, values, early_sums)
     reduce_pieces(RS_EARLY, 0)
-    finish_pieces(AG_EARLY, 0, piece_e)
     scaled_grad = last_hop(5)
     gate_grad = jnp.where(low128, scaled_grad * slope_r[...], part[...]).astype(BF16)
     by_reset = mm(turn(gate_grad)[:64, :].astype(BF16), states[...])
@@ -394,6 +413,7 @@
         ].astype(BF16)
     send_all(RS_LATE)
     outer, values = outer_hop(gate_grad, bg, 6)
+    finish_pieces(AG_EARLY, 0, piece_e)
     part[...] = upward[...] * gate_u[...] + scaled_grad * gate_r[...]
     inner_hop(gate_grad, bg, 6, outer, values, lambda: reduce_pieces(RS_LATE, 1))
     field[...] = field[...] + part[...]
@@ -459,9 +479,12 @@
             in_specs=[pl.BlockSpec(memory_space=pl.ANY)] * 10,
             out_specs=(vmem,) * 5,
             scratch_shapes=[
-                pltpu.VMEM((halo, 2 * width), BF16),
-                pltpu.VMEM((width, 2 * width), BF16),
-                pltpu.VMEM((width, 2 * halo), BF16),
+                pltpu.VMEM((2 * halo, width), BF16),
+                pltpu.VMEM((width, width), BF16),
+                pltpu.VMEM((width, width), BF16),
+                pltpu.VMEM((2 * width, halo), BF16),
+                pltpu.VMEM((2 * halo, halo), BF16),
+                pltpu.VMEM((2 * halo, halo), BF16),
                 pltpu.VMEM((width, 128), F32),
                 pltpu.VMEM((width, 128), F32),
                 pltpu.VMEM((width, 128), F32),
@@ -495,6 +518,7 @@
                 pltpu.VMEM((cols, 512), BF16),
                 pltpu.VMEM((8, 128), F32),
                 *[pltpu.VMEM((width, 128), F32)] * 6,
+                pltpu.VMEM((halo, 128), F32),
                 *(pltpu.VMEM(array.shape, array.dtype) for array in arrays),
                 pltpu.SemaphoreType.DMA((len(arrays),)),
             ],

time: 73.2 us -> 71.7 us (0.980)
  Pallas kernels: 72.4 us -> 70.9 us
    pallas_call x1, Pallas kernels: 70.7 us -> 69.2 us  [body(): pl.pallas_call(run, out_shape=(jax.ShapeDtypeStruct((1, hidden, width), B...]
where the time goes in v5:
time: 71.7 us; the launch traced here: 71.6 us
  Pallas kernels  70.9 us (99%)
    pallas_call x1, Pallas kernels, body(): pl.pallas_call(run, out_shape=(jax.ShapeDtypeStruct((1, hidden, width), B...  69.2 us
    pallas_call x1, Pallas kernels, body(): pl.pallas_call(write, out_shape=tuple((jax.ShapeDtypeStruct(array.shape,...  1.72 us

profile of v5, /device:TPU:1, one launch (start us, length us, event | category | flops | bytes accessed | tf_op | source)
XLA Modules:
  0.0 71.6 jit_solution(2033662191990732985)
XLA Ops:
  0.6 69.2 %shard_map.137 = (bf16[1,64,512]{2,1,0:T(8,128)(2,1)}, f32[330,128]{1,0:T(8,128)}, f32[1,128]{1,0:T(1,128)}, f32[64,330]{1,0:T(8,128)}, f32[1,64]{1,0:T(1,128)}) custom-call(bf16[1,2,512]{2,1,0:T(2,128)(2,1)} %refs_0_.1, bf16[1,64,512]{2,1,0:T(8,128)(2,1)} %refs_1_.1, bf16[1,64,512]{2,1,0:T(8,128)(2,1)} %refs_2_.1, bf16[330,128]{1,0:T(8,128)(2,1)} %bitcast.6, ...), custom_call_target="tpu_custom_call" | custom-call | tf_op jit(solution)/shard_map/pallas_call | solution.py:470
  69.9 1.7 %shard_map.138 = (bf16[1,64,512]{2,1,0:T(8,128)(2,1)}, f32[330,128]{1,0:T(8,128)}, f32[1,128]{1,0:T(1,128)}, f32[64,330]{1,0:T(8,128)}, f32[1,64]{1,0:T(1,128)}) custom-call(bf16[1,64,512]{2,1,0:T(8,128)(2,1)} %get-tuple-element.15.refs_0_, f32[330,128]{1,0:T(8,128)} %get-tuple-element.16.refs_1_, f32[1,128]{1,0:T(1,128)} %get-tuple-element.17.refs_2_, ...), custom_call_target="tpu_custom_call" | custom-call | tf_op jit(solution)/shard_map/pallas_call | solution.py:533

commit v6 on v5

--- a/solution.py
+++ b/solution.py
@@ -71,7 +71,7 @@
     sp, ml, wl, sw, comp_f, comp_a, held, upward, scale_f, scale_a, local, wide, states, mixed, field, wg, wc, bg, bc,
     send_w, recv_w, send_n, recv_n, ssem, rsem, osem, rows,
     early, late, piece_e, piece_l, snap_send, snap_recv, snap_s, snap_r, back_pick, pick, bias2,
-    gate_r, gate_u, slope_c, slope_r, part, inner_v, ahead,
+    gate_r, gate_u, slope_c, slope_r, part, inner_v, ahead, z_send, z_recv,
 ):
     me = lax.axis_index("dom")
     barrier = pltpu.get_barrier_semaphore()
@@ -94,8 +94,24 @@
 
     each_peer(lambda peer: pl.semaphore_signal(barrier, inc=1, device_id={"dom": peer}, device_id_type=MESH))
     mine = lax.axis_index("snap")
-    for k in range(1, n_snap):
-        pl.semaphore_signal(barrier, inc=1, device_id={"snap": (mine + k) % n_snap}, device_id_type=MESH)
+    plane = n_snap * NY * NC
+    my_place = (mine * NY + my_y) * NC + my_core
+
+    def each_mate(visit):
+        for dx in (2, 1, 3, 0):
+            for dy in (2, 1, 3, 0):
+                for dc in range(NC):
+                    if dx or dy or dc:
+                        x, y, c = (mine + dx) % n_snap, (my_y + dy) % NY, (my_core + dc) % NC
+                        visit((x * NY + y) * NC + c, {"snap": x, "dom": (y * NZ + my_z) * NC + c})
+
+    for dx in range(1, n_snap):
+        for dy in range(NY):
+            for dc in range(NC):
+                x, y, c = (mine + dx) % n_snap, (my_y + dy) % NY, (my_core + dc) % NC
+                pl.semaphore_signal(
+                    barrier, inc=1, device_id={"snap": x, "dom": (y * NZ + my_z) * NC + c}, device_id_type=MESH
+                )
 
     for copy in copies:
         copy.wait()
@@ -135,12 +151,12 @@
 
     def send_buf(hop):
         if hop >= HOPS:
-            return {RS_EARLY: early.at[0], RS_LATE: late.at[0]}[hop]
+            return early.at[0]
         return send_w.at[hop] if hop < 2 else send_n.at[hop - 2]
 
     def recv_buf(hop):
         if hop >= HOPS:
-            return {RS_EARLY: early.at[1], AG_EARLY: early.at[2], RS_LATE: late.at[1], AG_LATE: late.at[2]}[hop]
+            return early.at[1] if hop == RS_EARLY else early.at[2]
         return recv_w.at[hop] if hop < 2 else recv_n.at[hop - 2]
 
     def send_all(group):
@@ -182,7 +198,7 @@
             src.at[part].reshape(halo, 128)[...] = out[:, part * 128 : part * 128 + 128]
 
         if hop == 0:
-            pl.semaphore_wait(barrier, n_dom + n_snap - 2)
+            pl.semaphore_wait(barrier, n_dom - 1 + (n_snap - 1) * NY * NC)
         send_all(hop)
 
     def near(values):
@@ -227,9 +243,56 @@
             piece[part] = total[part * slots : (part + 1) * slots, :].astype(BF16)
         spread_piece(group, piece)
 
-    def gathered(group, tile, count):
-        at = tile * count
-        return recv_buf(group).at[at // halo].reshape(halo, 128)[at % halo : at % halo + count, :]
+    def gathered(tile):
+        at = tile * 128
+        return early.at[2, at // halo].reshape(halo, 128)[at % halo : at % halo + 128, :]
+
+    def late_send(group, piece_of):
+        dst = late.at[1] if group == RS_LATE else late.at[2]
+
+        def go(place, device):
+            pltpu.make_async_remote_copy(
+                piece_of(place), dst.at[my_place], ssem.at[group], rsem.at[group],
+                device_id=device, device_id_type=MESH,
+            ).start()
+
+        each_mate(go)
+        pltpu.make_async_copy(piece_of(my_place), dst.at[my_place], osem.at[group]).start()
+
+    def late_await(group):
+        dst = late.at[1] if group == RS_LATE else late.at[2]
+        rest = dst.at[pl.ds(0, plane - 1)]
+        pltpu.make_async_copy(rest, rest, rsem.at[group]).wait()
+        pltpu.make_async_copy(dst.at[my_place], dst.at[my_place], osem.at[group]).wait()
+
+    def z_copies():
+        for dz in (4, 3, 5, 2, 6, 1, 7):
+            yield pltpu.make_async_remote_copy(
+                z_send, z_recv.at[my_z], snap_s.at[1], snap_r.at[1],
+                device_id={"dom": (my_y * NZ + (my_z + dz) % NZ) * NC + my_core}, device_id_type=MESH,
+            )
+
+    def late_reduce():
+        late_await(RS_LATE)
+        rows_all = plane * 8
+        chosen = lanes(8, rows_all) % 8 == lax.broadcasted_iota(jnp.int32, (8, rows_all), 0)
+        total = mm(jnp.where(chosen, 1.0, 0.0).astype(BF16), late.at[1].reshape(rows_all, 128)[...])
+        z_send[...] = total
+        z_recv[my_z] = total
+        for copy in z_copies():
+            copy.start()
+
+    def late_finish():
+        others = z_recv.at[pl.ds(0, NZ - 1)]
+        pltpu.make_async_copy(others, others, snap_r.at[1]).wait()
+        total = z_recv[0]
+        for k in range(1, NZ):
+            total = total + z_recv[k]
+        piece_l[...] = total.astype(BF16)
+        late_send(AG_LATE, lambda place: piece_l)
+
+    def late_tile(tile):
+        return late.at[2].reshape(plane * 8, 128)[tile * 64 : tile * 64 + 64, :]
 
     def arrived(hop):
         dst = recv_buf(hop)
@@ -408,16 +471,16 @@
     gate_grad = jnp.where(low128, scaled_grad * slope_r[...], part[...]).astype(BF16)
     by_reset = mm(turn(gate_grad)[:64, :].astype(BF16), states[...])
     for tile in range(4):
-        late.at[0, 0].reshape(halo, 128)[tile * 64 : tile * 64 + 64, :] = by_reset[
+        late.at[0].reshape(plane * 8, 128)[tile * 64 : tile * 64 + 64, :] = by_reset[
             :, tile * 128 : tile * 128 + 128
         ].astype(BF16)
-    send_all(RS_LATE)
+    late_send(RS_LATE, lambda place: late.at[0, place])
     outer, values = outer_hop(gate_grad, bg, 6)
     finish_pieces(AG_EARLY, 0, piece_e)
     part[...] = upward[...] * gate_u[...] + scaled_grad * gate_r[...]
-    inner_hop(gate_grad, bg, 6, outer, values, lambda: reduce_pieces(RS_LATE, 1))
+    inner_hop(gate_grad, bg, 6, outer, values, late_reduce)
     field[...] = field[...] + part[...]
-    finish_pieces(AG_LATE, 1, piece_l)
+    late_finish()
 
     await_recv(AG_EARLY)
     bias_row = jnp.where(lanes(8, 128) == 64 + fin, 1.0, 0.0).astype(BF16)
@@ -425,16 +488,16 @@
     def put_bias(tiles, bias_out):
         bias_out[...] = mm_t1(bias_row, tiles[2])[0:1, :] * factor
 
-    tiles = [gathered(AG_EARLY, tile, 128)[:64] for tile in range(4)]
+    tiles = [gathered(tile)[:64] for tile in range(4)]
     total = mm(tiles[0], back_pick[:128, :])
     for tile in range(1, 4):
         total = total + mm(tiles[tile], back_pick[tile * 128 : tile * 128 + 128, :])
     cand_out[...] = total * factor
     put_bias(tiles, cand_bias_out)
     state_ref[0] = jnp.transpose(last_hop(7))[:64, :].astype(BF16)
-    await_recv(AG_LATE)
+    late_await(AG_LATE)
     tiles = [
-        jnp.concatenate([gathered(AG_LATE, tile, 64), gathered(AG_EARLY, tile, 128)[64:]], axis=0)
+        jnp.concatenate([late_tile(tile), gathered(tile)[64:]], axis=0)
         for tile in range(4)
     ]
     total = mm_t1(pick[:, :128], tiles[0])
@@ -443,12 +506,16 @@
     gate_out[...] = total * factor
     put_bias(tiles, gate_bias_out)
 
-    for group in range(GROUPS):
+    for group in range(RS_LATE):
         rest = recv_buf(group).at[:, pl.ds(0, n_dom - 1)]
         pltpu.make_async_copy(rest, rest, ssem.at[group]).wait()
-    for which in range(2):
-        others = snap_recv.at[which, pl.ds(0, n_snap - 1)]
-        pltpu.make_async_copy(others, others, snap_s.at[which]).wait()
+    for group in (RS_LATE, AG_LATE):
+        rest = late.at[2, pl.ds(0, plane - 1)]
+        pltpu.make_async_copy(rest, rest, ssem.at[group]).wait()
+    others = snap_recv.at[0, pl.ds(0, n_snap - 1)]
+    pltpu.make_async_copy(others, others, snap_s.at[0]).wait()
+    others = z_recv.at[pl.ds(0, NZ - 1)]
+    pltpu.make_async_copy(others, others, snap_s.at[1]).wait()
 
 
 def solution(mesh):
@@ -507,9 +574,9 @@
                 pltpu.SemaphoreType.DMA((GROUPS,)),
                 pltpu.VMEM((2, 128, width), F32),
                 pltpu.VMEM((3, 2, n_dom, slots, 128), BF16),
-                pltpu.VMEM((3, 1, n_dom, slots, 128), BF16),
+                pltpu.VMEM((3, n_snap * NY * NC, 8, 128), BF16),
                 pltpu.VMEM((2, slots, 128), BF16),
-                pltpu.VMEM((1, slots, 128), BF16),
+                pltpu.VMEM((8, 128), BF16),
                 pltpu.VMEM((2, 8, 128), F32),
                 pltpu.VMEM((2, n_snap, 8, 128), F32),
                 pltpu.SemaphoreType.DMA((2,)),
@@ -519,6 +586,8 @@
                 pltpu.VMEM((8, 128), F32),
                 *[pltpu.VMEM((width, 128), F32)] * 6,
                 pltpu.VMEM((halo, 128), F32),
+                pltpu.VMEM((8, 128), F32),
+                pltpu.VMEM((NZ, 8, 128), F32),
                 *(pltpu.VMEM(array.shape, array.dtype) for array in arrays),
                 pltpu.SemaphoreType.DMA((len(arrays),)),
             ],

time: 71.7 us -> 70.4 us (0.982)
  Pallas kernels: 70.9 us -> 69.6 us
    pallas_call x1, Pallas kernels: 69.2 us -> 67.9 us  [body(): pl.pallas_call(run, out_shape=(jax.ShapeDtypeStruct((1, hidden, width), B...]
where the time goes in v6:
time: 70.4 us; the launch traced here: 70.3 us
  Pallas kernels  69.6 us (99%)
    pallas_call x1, Pallas kernels, body(): pl.pallas_call(run, out_shape=(jax.ShapeDtypeStruct((1, hidden, width), B...  67.9 us
    pallas_call x1, Pallas kernels, body(): pl.pallas_call(write, out_shape=tuple((jax.ShapeDtypeStruct(array.shape,...  1.72 us

profile of v6, /device:TPU:1, one launch (start us, length us, event | category | flops | bytes accessed | tf_op | source)
XLA Modules:
  0.0 70.3 jit_solution(8042069807599493270)
XLA Ops:
  0.6 67.9 %shard_map.137 = (bf16[1,64,512]{2,1,0:T(8,128)(2,1)}, f32[330,128]{1,0:T(8,128)}, f32[1,128]{1,0:T(1,128)}, f32[64,330]{1,0:T(8,128)}, f32[1,64]{1,0:T(1,128)}) custom-call(bf16[1,2,512]{2,1,0:T(2,128)(2,1)} %refs_0_.1, bf16[1,64,512]{2,1,0:T(8,128)(2,1)} %refs_1_.1, bf16[1,64,512]{2,1,0:T(8,128)(2,1)} %refs_2_.1, bf16[330,128]{1,0:T(8,128)(2,1)} %bitcast.6, ...), custom_call_target="tpu_custom_call" | custom-call | tf_op jit(solution)/shard_map/pallas_call | solution.py:537
  68.6 1.7 %shard_map.138 = (bf16[1,64,512]{2,1,0:T(8,128)(2,1)}, f32[330,128]{1,0:T(8,128)}, f32[1,128]{1,0:T(1,128)}, f32[64,330]{1,0:T(8,128)}, f32[1,64]{1,0:T(1,128)}) custom-call(bf16[1,64,512]{2,1,0:T(8,128)(2,1)} %get-tuple-element.15.refs_0_, f32[330,128]{1,0:T(8,128)} %get-tuple-element.16.refs_1_, f32[1,128]{1,0:T(1,128)} %get-tuple-element.17.refs_2_, ...), custom_call_target="tpu_custom_call" | custom-call | tf_op jit(solution)/shard_map/pallas_call | solution.py:602

commit v7 on v6

--- a/solution.py
+++ b/solution.py
@@ -70,7 +70,7 @@
     state_ref, gate_out, gate_bias_out, cand_out, cand_bias_out,
     sp, ml, wl, sw, comp_f, comp_a, held, upward, scale_f, scale_a, local, wide, states, mixed, field, wg, wc, bg, bc,
     send_w, recv_w, send_n, recv_n, ssem, rsem, osem, rows,
-    early, late, piece_e, piece_l, snap_send, snap_recv, snap_s, snap_r, back_pick, pick, bias2,
+    early, late, piece_e, piece_l, z_send_e, z_recv_e, snap_s, snap_r, back_pick, pick, bias2,
     gate_r, gate_u, slope_c, slope_r, part, inner_v, ahead, z_send, z_recv,
 ):
     me = lax.axis_index("dom")
@@ -150,13 +150,9 @@
     deg_rest = deg_halo - deg_high
 
     def send_buf(hop):
-        if hop >= HOPS:
-            return early.at[0]
         return send_w.at[hop] if hop < 2 else send_n.at[hop - 2]
 
     def recv_buf(hop):
-        if hop >= HOPS:
-            return early.at[1] if hop == RS_EARLY else early.at[2]
         return recv_w.at[hop] if hop < 2 else recv_n.at[hop - 2]
 
     def send_all(group):
@@ -170,18 +166,6 @@
 
         each_peer(go)
         pltpu.make_async_copy(src.at[:, me], dst.at[:, me], osem.at[group]).start()
-
-    def spread_piece(group, src):
-        dst = recv_buf(group)
-
-        def go(peer):
-            pltpu.make_async_remote_copy(
-                src, dst.at[:, me], ssem.at[group], rsem.at[group],
-                device_id={"dom": peer}, device_id_type=MESH,
-            ).start()
-
-        each_peer(go)
-        pltpu.make_async_copy(src, dst.at[:, me], osem.at[group]).start()
 
     def to_send(values):
         rows = mm(sp[...], values)
@@ -211,44 +195,11 @@
         pltpu.make_async_copy(rest, rest, rsem.at[hop]).wait()
         pltpu.make_async_copy(dst.at[:, me], dst.at[:, me], osem.at[hop]).wait()
 
-    def reduce_pieces(group, which):
-        await_recv(group)
-        dst = recv_buf(group)
-        parts = dst.shape[0]
-        row = lax.broadcasted_iota(jnp.int32, (8, halo * parts), 0)
-        col = lanes(8, halo * parts)
-        slots = dst.shape[2]
-        chosen = (col % slots == row % slots) & (col // halo == (row // slots) % parts)
-        chosen = jnp.where(chosen, 1.0, 0.0).astype(BF16)
-        terms = [dst.at[part].reshape(halo, 128)[...] for part in range(parts)]
-        total = mm(chosen[:, :halo], terms[0])
-        for part in range(1, parts):
-            total = total + mm(chosen[:, part * halo : part * halo + halo], terms[part])
-        snap_send[which] = total
-        snap_recv[which, mine] = total
-        for k in range(1, n_snap):
-            pltpu.make_async_remote_copy(
-                snap_send.at[which], snap_recv.at[which, mine], snap_s.at[which], snap_r.at[which],
-                device_id={"snap": (mine + k) % n_snap}, device_id_type=MESH,
-            ).start()
-
-    def finish_pieces(group, which, piece):
-        others = snap_recv.at[which, pl.ds(0, n_snap - 1)]
-        pltpu.make_async_copy(others, others, snap_r.at[which]).wait()
-        total = snap_recv[which, 0]
-        for k in range(1, n_snap):
-            total = total + snap_recv[which, k]
-        slots = piece.shape[1]
-        for part in range(piece.shape[0]):
-            piece[part] = total[part * slots : (part + 1) * slots, :].astype(BF16)
-        spread_piece(group, piece)
-
-    def gathered(tile):
-        at = tile * 128
-        return early.at[2, at // halo].reshape(halo, 128)[at % halo : at % halo + 128, :]
-
-    def late_send(group, piece_of):
-        dst = late.at[1] if group == RS_LATE else late.at[2]
+    def tile_rows(buf, tile, count):
+        return buf.at[2].reshape(plane * buf.shape[2], 128)[tile * count : tile * count + count, :]
+
+    def plane_send(group, buf, slot, piece_of):
+        dst = buf.at[slot]
 
         def go(place, device):
             pltpu.make_async_remote_copy(
@@ -259,40 +210,35 @@
         each_mate(go)
         pltpu.make_async_copy(piece_of(my_place), dst.at[my_place], osem.at[group]).start()
 
-    def late_await(group):
-        dst = late.at[1] if group == RS_LATE else late.at[2]
+    def plane_await(group, buf, slot):
+        dst = buf.at[slot]
         rest = dst.at[pl.ds(0, plane - 1)]
         pltpu.make_async_copy(rest, rest, rsem.at[group]).wait()
         pltpu.make_async_copy(dst.at[my_place], dst.at[my_place], osem.at[group]).wait()
 
-    def z_copies():
+    def reduce_pieces(group, buf, which, mine_z, all_z):
+        plane_await(group, buf, 1)
+        height = buf.shape[2]
+        rows_all = plane * height
+        chosen = lanes(height, rows_all) % height == lax.broadcasted_iota(jnp.int32, (height, rows_all), 0)
+        total = mm(jnp.where(chosen, 1.0, 0.0).astype(BF16), buf.at[1].reshape(rows_all, 128)[...])
+        mine_z[...] = total
+        all_z[my_z] = total
         for dz in (4, 3, 5, 2, 6, 1, 7):
-            yield pltpu.make_async_remote_copy(
-                z_send, z_recv.at[my_z], snap_s.at[1], snap_r.at[1],
+            pltpu.make_async_remote_copy(
+                mine_z, all_z.at[my_z], snap_s.at[which], snap_r.at[which],
                 device_id={"dom": (my_y * NZ + (my_z + dz) % NZ) * NC + my_core}, device_id_type=MESH,
-            )
-
-    def late_reduce():
-        late_await(RS_LATE)
-        rows_all = plane * 8
-        chosen = lanes(8, rows_all) % 8 == lax.broadcasted_iota(jnp.int32, (8, rows_all), 0)
-        total = mm(jnp.where(chosen, 1.0, 0.0).astype(BF16), late.at[1].reshape(rows_all, 128)[...])
-        z_send[...] = total
-        z_recv[my_z] = total
-        for copy in z_copies():
-            copy.start()
-
-    def late_finish():
-        others = z_recv.at[pl.ds(0, NZ - 1)]
-        pltpu.make_async_copy(others, others, snap_r.at[1]).wait()
-        total = z_recv[0]
+            ).start()
+
+    def finish_pieces(group, buf, which, all_z, piece):
+        others = all_z.at[pl.ds(0, NZ - 1)]
+        pltpu.make_async_copy(others, others, snap_r.at[which]).wait()
+        total = all_z[0]
         for k in range(1, NZ):
-            total = total + z_recv[k]
-        piece_l[...] = total.astype(BF16)
-        late_send(AG_LATE, lambda place: piece_l)
-
-    def late_tile(tile):
-        return late.at[2].reshape(plane * 8, 128)[tile * 64 : tile * 64 + 64, :]
+            total = total + all_z[k]
+        piece[...] = total.astype(BF16)
+        plane_send(group, buf, 2, lambda place: piece)
+
 
     def arrived(hop):
         dst = recv_buf(hop)
@@ -458,15 +404,15 @@
         by_cand = mm(grads[:64, :], mixed[...])
         by_update = mm(grads[64:, :], states[...])
         for tile in range(4):
-            dst = early.at[0, tile // 2].reshape(halo, 128)
-            at = tile % 2 * 128
+            dst = early.at[0].reshape(plane * 16, 128)
+            at = tile * 128
             dst[at : at + 64, :] = by_cand[:, tile * 128 : tile * 128 + 128].astype(BF16)
             dst[at + 64 : at + 128, :] = by_update[:, tile * 128 : tile * 128 + 128].astype(BF16)
-        send_all(RS_EARLY)
+        plane_send(RS_EARLY, early, 1, lambda place: early.at[0, place])
 
     outer, values = outer_hop(cand_grad, bc, 4)
     inner_hop(cand_grad, bc, 4, outer, values, early_sums)
-    reduce_pieces(RS_EARLY, 0)
+    reduce_pieces(RS_EARLY, early, 0, z_send_e, z_recv_e)
     scaled_grad = last_hop(5)
     gate_grad = jnp.where(low128, scaled_grad * slope_r[...], part[...]).astype(BF16)
     by_reset = mm(turn(gate_grad)[:64, :].astype(BF16), states[...])
@@ -474,30 +420,30 @@
         late.at[0].reshape(plane * 8, 128)[tile * 64 : tile * 64 + 64, :] = by_reset[
             :, tile * 128 : tile * 128 + 128
         ].astype(BF16)
-    late_send(RS_LATE, lambda place: late.at[0, place])
+    plane_send(RS_LATE, late, 1, lambda place: late.at[0, place])
     outer, values = outer_hop(gate_grad, bg, 6)
-    finish_pieces(AG_EARLY, 0, piece_e)
+    finish_pieces(AG_EARLY, early, 0, z_recv_e, piece_e)
     part[...] = upward[...] * gate_u[...] + scaled_grad * gate_r[...]
-    inner_hop(gate_grad, bg, 6, outer, values, late_reduce)
+    inner_hop(gate_grad, bg, 6, outer, values, lambda: reduce_pieces(RS_LATE, late, 1, z_send, z_recv))
     field[...] = field[...] + part[...]
-    late_finish()
-
-    await_recv(AG_EARLY)
+    finish_pieces(AG_LATE, late, 1, z_recv, piece_l)
+
+    plane_await(AG_EARLY, early, 2)
     bias_row = jnp.where(lanes(8, 128) == 64 + fin, 1.0, 0.0).astype(BF16)
 
     def put_bias(tiles, bias_out):
         bias_out[...] = mm_t1(bias_row, tiles[2])[0:1, :] * factor
 
-    tiles = [gathered(tile)[:64] for tile in range(4)]
+    tiles = [tile_rows(early, tile, 128)[:64] for tile in range(4)]
     total = mm(tiles[0], back_pick[:128, :])
     for tile in range(1, 4):
         total = total + mm(tiles[tile], back_pick[tile * 128 : tile * 128 + 128, :])
     cand_out[...] = total * factor
     put_bias(tiles, cand_bias_out)
     state_ref[0] = jnp.transpose(last_hop(7))[:64, :].astype(BF16)
-    late_await(AG_LATE)
+    plane_await(AG_LATE, late, 2)
     tiles = [
-        jnp.concatenate([late_tile(tile), gathered(tile)[64:]], axis=0)
+        jnp.concatenate([tile_rows(late, tile, 64), tile_rows(early, tile, 128)[64:]], axis=0)
         for tile in range(4)
     ]
     total = mm_t1(pick[:, :128], tiles[0])
@@ -506,16 +452,15 @@
     gate_out[...] = total * factor
     put_bias(tiles, gate_bias_out)
 
-    for group in range(RS_LATE):
+    for group in range(HOPS):
         rest = recv_buf(group).at[:, pl.ds(0, n_dom - 1)]
         pltpu.make_async_copy(rest, rest, ssem.at[group]).wait()
-    for group in (RS_LATE, AG_LATE):
-        rest = late.at[2, pl.ds(0, plane - 1)]
+    for group, buf in ((RS_EARLY, early), (AG_EARLY, early), (RS_LATE, late), (AG_LATE, late)):
+        rest = buf.at[2, pl.ds(0, plane - 1)]
         pltpu.make_async_copy(rest, rest, ssem.at[group]).wait()
-    others = snap_recv.at[0, pl.ds(0, n_snap - 1)]
-    pltpu.make_async_copy(others, others, snap_s.at[0]).wait()
-    others = z_recv.at[pl.ds(0, NZ - 1)]
-    pltpu.make_async_copy(others, others, snap_s.at[1]).wait()
+    for which, all_z in ((0, z_recv_e), (1, z_recv)):
+        others = all_z.at[pl.ds(0, NZ - 1)]
+        pltpu.make_async_copy(others, others, snap_s.at[which]).wait()
 
 
 def solution(mesh):
@@ -573,12 +518,12 @@
                 pltpu.SemaphoreType.DMA((GROUPS,)),
                 pltpu.SemaphoreType.DMA((GROUPS,)),
                 pltpu.VMEM((2, 128, width), F32),
-                pltpu.VMEM((3, 2, n_dom, slots, 128), BF16),
+                pltpu.VMEM((3, n_snap * NY * NC, 16, 128), BF16),
                 pltpu.VMEM((3, n_snap * NY * NC, 8, 128), BF16),
-                pltpu.VMEM((2, slots, 128), BF16),
+                pltpu.VMEM((16, 128), BF16),
                 pltpu.VMEM((8, 128), BF16),
-                pltpu.VMEM((2, 8, 128), F32),
-                pltpu.VMEM((2, n_snap, 8, 128), F32),
+                pltpu.VMEM((16, 128), F32),
+                pltpu.VMEM((NZ, 16, 128), F32),
                 pltpu.SemaphoreType.DMA((2,)),
                 pltpu.SemaphoreType.DMA((2,)),
                 pltpu.VMEM((512, cols), BF16),

time: 70.4 us -> 70.6 us (level)
  no operation moved by 1% of the time
where the time goes in v7:
time: 70.6 us; the launch traced here: 70.4 us
  Pallas kernels  69.8 us (99%)
    pallas_call x1, Pallas kernels, body(): pl.pallas_call(run, out_shape=(jax.ShapeDtypeStruct((1, hidden, width), B...  68.1 us
    pallas_call x1, Pallas kernels, body(): pl.pallas_call(write, out_shape=tuple((jax.ShapeDtypeStruct(array.shape,...  1.72 us

profile of v7, /device:TPU:1, one launch (start us, length us, event | category | flops | bytes accessed | tf_op | source)
XLA Modules:
  0.0 70.4 jit_solution(6200003796564569613)
XLA Ops:
  0.6 68.1 %shard_map.137 = (bf16[1,64,512]{2,1,0:T(8,128)(2,1)}, f32[330,128]{1,0:T(8,128)}, f32[1,128]{1,0:T(1,128)}, f32[64,330]{1,0:T(8,128)}, f32[1,64]{1,0:T(1,128)}) custom-call(bf16[1,2,512]{2,1,0:T(2,128)(2,1)} %refs_0_.1, bf16[1,64,512]{2,1,0:T(8,128)(2,1)} %refs_1_.1, bf16[1,64,512]{2,1,0:T(8,128)(2,1)} %refs_2_.1, bf16[330,128]{1,0:T(8,128)(2,1)} %bitcast.6, ...), custom_call_target="tpu_custom_call" | custom-call | tf_op jit(solution)/shard_map/pallas_call | solution.py:482
  68.7 1.7 %shard_map.138 = (bf16[1,64,512]{2,1,0:T(8,128)(2,1)}, f32[330,128]{1,0:T(8,128)}, f32[1,128]{1,0:T(1,128)}, f32[64,330]{1,0:T(8,128)}, f32[1,64]{1,0:T(1,128)}) custom-call(bf16[1,64,512]{2,1,0:T(8,128)(2,1)} %get-tuple-element.15.refs_0_, f32[330,128]{1,0:T(8,128)} %get-tuple-element.16.refs_1_, f32[1,128]{1,0:T(1,128)} %get-tuple-element.17.refs_2_, ...), custom_call_target="tpu_custom_call" | custom-call | tf_op jit(solution)/shard_map/pallas_call | solution.py:547
